TPU v7x, 128 devices: a whole 4x4x4 slice. The times are simulated.
128 devices in a mesh: row: 16 (over z, y), ga: 8 (over x, core).
Axes of the slice: x: 4, y: 4, z: 4, core: 2. Of those that a mesh axis runs over, the one named last changes fastest.
Arguments:
- fine_feats: bfloat16 [15360, 64, 512], P(('row', 'ga')), may hold values from -6 to 6
- fine_child: int32 [15360], P(('row', 'ga')), may hold values from -1 to 511, as said below
- parent_block: int32 [1024], P(('row', 'ga')), may hold values from 0 to 63, as said below
- w_parent: bfloat16 [64, 128], replicated, may hold values from -2 to 2
- w_root_in: bfloat16 [128, 256], replicated, may hold values from -1.5 to 1.5
- w_root: bfloat16 [256, 256, 3, 3, 3], P('ga'), may hold values from -0.15625 to 0.15625
- root_bias: float32 [256], P('ga'), may hold values from -0.5 to 0.5
- w_down: bfloat16 [256, 128], replicated, may hold values from -0.375 to 0.375
- w_skip: bfloat16 [128, 64], replicated, may hold values from -0.5 to 0.5
Outputs:
- fine_out: bfloat16 [15360, 64, 512], P(('row', 'ga'))
- root_features: bfloat16 [256, 64, 32, 32], P('ga', 'row')
Inputs may be any that keep to these rules, and one draw needn't show every extreme that they name: `fine_child`: parents i * 8 to (i + 1) * 8 - 1 of a region belong to the region's device of ga index i. Over the slots of a region every child index 0 to 511 appears exactly once. The slots of one device hold at most 15 children of one device's parents, and in every region some device holds exactly 15 children of each device's parents. `parent_block`: the parents of one region have distinct places.
All inputs are finite; a program needn't handle non-finite values.
Results may differ from a plain program's by a relative error of at most 0.013.
Values may be sent and summed in bfloat16 or wider, within the bound.
A program may use at most 128 MiB of HBM per device.

v0:
```python
import functools

import jax
import jax.numpy as jnp
from jax import lax
from jax.experimental import pallas as pl
from jax.experimental.pallas import tpu as pltpu
from jax.sharding import PartitionSpec as P

BF = jnp.bfloat16
F32 = jnp.float32
I32 = jnp.int32
MESH = pl.DeviceIdType.MESH
SLOTS = 120
NB = 4
SB = 32
TB = 24


def iota(shape, dim):
    return lax.broadcasted_iota(I32, shape, dim)


def column_of(v):
    z, y, x = v >> 6, (v >> 3) & 7, v & 7
    w = (z >> 2) * 4 + (y >> 2) * 2 + (x >> 2)
    g = ((z >> 1) & 1) * 4 + ((y >> 1) & 1) * 2 + ((x >> 1) & 1)
    return g * 8 + w


def nt(a, b):
    return lax.dot_general(a, b, (((1,), (1,)), ((), ())), preferred_element_type=F32)


def tn(a, b):
    return lax.dot_general(a, b, (((0,), (0,)), ((), ())), preferred_element_type=F32)


def mm(a, b):
    return jnp.dot(a, b, preferred_element_type=F32)


def root_kernel(
    rows,
    child_ref,
    block_ref,
    x_hbm,
    wp_ref,
    win_ref,
    wc_ref,
    bias_ref,
    hid_hbm,
    back_hbm,
    nat_ref,
    xbuf,
    p8,
    hid,
    pp,
    ints,
    gathered,
    place,
    slab,
    halo,
    xt,
    taps,
    rft,
    quad,
    perm,
    msgs,
    x_sem,
    hid_sem,
    int_send,
    int_recv,
    ag_send,
    ag_recv,
    fw_send,
    fw_recv,
    halo_send,
    halo_recv,
    back_send,
    back_recv,
    own_sem,
):
    row = lax.axis_index("row")
    me = lax.axis_index("ga")
    chip = me // 2
    core = lax.rem(me, 2)
    partner = 2 * chip + 1 - core
    last = rows - 1

    def peer(k):
        return lax.rem(me + k, 8)

    def chip_peer(k):
        return 2 * lax.rem(chip + k, 4) + core

    def at(ga):
        return (row, ga)

    x_copies = []
    for blk in range(NB):
        n = min(SB, SLOTS - blk * SB)
        x_copies.append(
            pltpu.make_async_copy(
                x_hbm.at[pl.ds(blk * SB, n)], xbuf.at[blk, pl.ds(0, n)], x_sem.at[blk]
            )
        )
        x_copies[-1].start()
    tail = SLOTS - (NB - 1) * SB
    xbuf[NB - 1, tail:] = jnp.zeros((SB - tail, 64, 512), BF)

    barrier = pltpu.get_barrier_semaphore()
    for k in range(1, 8):
        pl.semaphore_signal(barrier, inc=1, device_id=at(peer(k)), device_id_type=MESH)

    @pl.when(row > 0)
    def _():
        pl.semaphore_signal(barrier, inc=1, device_id=(row - 1, me), device_id_type=MESH)

    @pl.when(row < last)
    def _():
        pl.semaphore_signal(barrier, inc=1, device_id=(row + 1, me), device_id_type=MESH)

    ints[me] = jnp.full((8, 128), -1, I32)
    ints[me, 0:1, 0:SLOTS] = child_ref[...]
    ints[me, 1:2, 0:8] = block_ref[...]
    where = column_of(iota((512, 256), 0))
    lane = iota((512, 256), 1)
    for k in range(4):
        p8[k] = jnp.where(lane == where + 64 * k, 0.125, 0.0).astype(BF)

    sides = (row > 0).astype(I32) + (row < last).astype(I32)
    pl.semaphore_wait(barrier, 7 + sides)

    int_copies = []
    for k in range(1, 8):
        int_copies.append(
            pltpu.make_async_remote_copy(
                ints.at[me],
                ints.at[me],
                int_send.at[k],
                int_recv.at[k],
                device_id=at(peer(k)),
                device_id_type=MESH,
            )
        )
        int_copies[-1].start()

    def piece(ga, blk):
        return gathered.at[pl.ds(pl.multiple_of(ga * 128 + blk * SB, SB), SB)]

    hid_copies, ag_copies, fw_copies = [], [], []
    for blk in range(NB):
        x_copies[blk].wait()
        pooled = None
        for k in range(4):
            x = jnp.concatenate([xbuf[blk, 4 * g + k] for g in range(SB // 4)], axis=0)
            part = mm(x, p8[k])
            pooled = part if pooled is None else pooled + part
        pooled = pooled.astype(BF)
        for g in range(SB // 4):
            h = tn(pooled[g * 64 : (g + 1) * 64], wp_ref[...])
            h = jnp.maximum(h, 0.0).astype(BF)
            hid[pl.ds((blk * SB + 4 * g) * 64, 256), :] = h
            mean = jnp.sum(h.astype(F32).reshape(4, 8, 8, 128), axis=1) * 0.125
            pp[pl.ds(g * 32, 32), :] = mean.reshape(32, 128)
        start = pl.multiple_of(me * 128 + blk * SB, SB)
        for w in range(8):
            gathered[pl.ds(start, SB), w * 128 : (w + 1) * 128] = pp[
                pl.ds(w, SB, stride=8), :
            ].astype(BF)
        n = min(SB, SLOTS - blk * SB)
        hid_copies.append(
            pltpu.make_async_copy(
                hid.at[pl.ds(blk * SB * 64, n * 64)],
                hid_hbm.at[pl.ds(blk * SB * 64, n * 64)],
                hid_sem.at[blk],
            )
        )
        hid_copies[-1].start()
        for k in (2, 1, 3):
            ag_copies.append(
                pltpu.make_async_remote_copy(
                    piece(me, blk),
                    piece(me, blk),
                    ag_send.at[blk, k],
                    ag_recv.at[blk, k],
                    device_id=at(chip_peer(k)),
                    device_id_type=MESH,
                )
            )
            ag_copies[-1].start()
        fw_copies.append(
            pltpu.make_async_remote_copy(
                piece(me, blk),
                piece(me, blk),
                fw_send.at[blk, 0],
                fw_recv.at[blk, 0],
                device_id=at(partner),
                device_id_type=MESH,
            )
        )
        fw_copies[-1].start()

    for k in range(1, 8):
        int_copies[k - 1].wait()
    child = jnp.concatenate([ints[m, 0:1, :] for m in range(8)], axis=0)
    parent = child >> 3
    block = jnp.zeros((8, 128), I32)
    for m in range(8):
        blocks = ints[m, 1:2, :]
        for i in range(8):
            block = jnp.where(parent == 8 * m + i, blocks[:, i : i + 1], block)
    octant = child & 7
    pos = (
        (octant >> 2) * 256
        + (2 * (block >> 3) + ((octant >> 1) & 1)) * 16
        + 2 * (block & 7)
        + (octant & 1)
    )
    pos = jnp.where(child >= 0, pos, -1)
    for m in range(8):
        hot = iota((512, 128), 0) == pos[m : m + 1, :]
        place[:, m * 128 : (m + 1) * 128] = jnp.where(hot, 1.0, 0.0).astype(BF)
    for c in range(4):
        p = iota((1024, 256), 0)
        q = iota((1024, 256), 1) + 256 * c
        iy, ix, oy, ox = p >> 9, (p >> 8) & 1, (p >> 4) & 15, p & 15
        hot = q == (2 * oy + iy) * 32 + 2 * ox + ix
        perm[:, c * 256 : (c + 1) * 256] = jnp.where(hot, 1.0, 0.0).astype(BF)

    for blk in range(NB):
        for k in (1, 3, 2):
            src = chip_peer(4 - k)
            pltpu.make_async_remote_copy(
                piece(me, blk),
                piece(src, blk),
                ag_send.at[blk, k],
                ag_recv.at[blk, k],
                device_id=at(partner),
                device_id_type=MESH,
            ).wait_recv()
            fw_copies.append(
                pltpu.make_async_remote_copy(
                    piece(src, blk),
                    piece(src, blk),
                    fw_send.at[blk, k],
                    fw_recv.at[blk, k],
                    device_id=at(partner),
                    device_id_type=MESH,
                )
            )
            fw_copies[-1].start()
    for c in fw_copies:
        c.wait_recv()

    for i in range(4):
        slab[:, i * 256 : (i + 1) * 256] = mm(
            place[...], gathered[:, i * 256 : (i + 1) * 256]
        ).astype(BF)

    low = pltpu.make_async_remote_copy(
        slab.at[pl.ds(0, 256), pl.ds(0, 512)],
        halo.at[1],
        halo_send.at[0],
        halo_recv.at[1],
        device_id=(jnp.maximum(row - 1, 0), me),
        device_id_type=MESH,
    )
    high = pltpu.make_async_remote_copy(
        slab.at[pl.ds(256, 256), pl.ds(512, 512)],
        halo.at[0],
        halo_send.at[1],
        halo_recv.at[0],
        device_id=(jnp.minimum(row + 1, last), me),
        device_id_type=MESH,
    )

    @pl.when(row > 0)
    def _():
        low.start()

    @pl.when(row < last)
    def _():
        high.start()

    win = win_ref[...]
    for w in range(8):
        r = mm(slab[:, w * 128 : (w + 1) * 128], win).astype(BF)
        for oz in range(2):
            xt[1 + 2 * oz + (w >> 2), w & 3] = r[oz * 256 : (oz + 1) * 256]

    spot = iota((32, 256), 1)
    oy, ox = spot >> 4, spot & 15
    bias = jnp.sum(
        jnp.where(iota((32, 32), 0) == iota((32, 32), 1), bias_ref[...], 0.0),
        axis=1,
        keepdims=True,
    )

    def convolve(z):
        for ab in range(4):
            acc = None
            for dz in range(3):
                part = nt(wc_ref[dz * 288 : (dz + 1) * 288], xt[z + dz, ab])
                acc = part if acc is None else acc + part
            taps[ab] = acc

        def tap(a, b, dy, dx):
            t = ((dy + 1) * 3 + dx + 1) * 32
            return taps[2 * a + b, t : t + 32, :]

        for iy in range(2):
            for ix in range(2):
                ys = [(iy, 0), (1 - iy, 1 - 2 * iy)]
                xs = [(ix, 0), (1 - ix, 1 - 2 * ix)]
                ysh = (1 - iy, 2 * iy - 1)
                xsh = (1 - ix, 2 * ix - 1)
                by, bx = (15, 15)
                plain = sum(tap(a, b, dy, dx) for a, dy in ys for b, dx in xs)
                only_x = sum(tap(a, xsh[0], dy, xsh[1]) for a, dy in ys)
                only_y = sum(tap(ysh[0], b, ysh[1], dx) for b, dx in xs)
                both = tap(ysh[0], xsh[0], ysh[1], xsh[1])

                def shift_x(v):
                    v = pltpu.roll(v, 255 if ix else 1, 1)
                    return jnp.where(ox == (bx if ix else 0), 0.0, v)

                def shift_y(v):
                    v = pltpu.roll(v, 240 if iy else 16, 1)
                    return jnp.where(oy == (by if iy else 0), 0.0, v)

                total = plain + shift_x(only_x) + shift_y(only_y + shift_x(both))
                out = jnp.maximum(total + bias, 0.0).astype(BF)
                w = (z & 1) * 4 + iy * 2 + ix
                rft[w * 32 : (w + 1) * 32, (z >> 1) * 256 : ((z >> 1) + 1) * 256] = out
                c = iy * 2 + ix
                quad[z * 32 : (z + 1) * 32, c * 256 : (c + 1) * 256] = out

    convolve(1)
    convolve(2)

    @pl.when(row > 0)
    def _():
        high.wait_recv()

    @pl.when(row < last)
    def _():
        low.wait_recv()

    @pl.when(row == 0)
    def _():
        halo[0] = jnp.zeros((256, 512), BF)

    @pl.when(row == last)
    def _():
        halo[1] = jnp.zeros((256, 512), BF)

    for side in range(2):
        for c in range(4):
            xt[5 * side, c] = mm(halo[side, :, c * 128 : (c + 1) * 128], win).astype(BF)
    convolve(0)
    convolve(3)

    for i in range(4):
        m2 = mm(rft[...], place[:, i * 256 : (i + 1) * 256]).astype(BF)
        msgs[2 * i] = m2[:, :128]
        msgs[2 * i + 1] = m2[:, 128:]
    back_copies = []
    for k in (4, 3, 5, 2, 6, 1, 7):
        back_copies.append(
            pltpu.make_async_remote_copy(
                msgs.at[peer(k)],
                back_hbm.at[me],
                back_send.at[k],
                back_recv.at[k],
                device_id=at(peer(k)),
                device_id_type=MESH,
            )
        )
        back_copies[-1].start()
    own = pltpu.make_async_copy(msgs.at[me], back_hbm.at[me], own_sem)
    own.start()

    for i in range(4):
        n4 = mm(quad[...], perm[:, i * 256 : (i + 1) * 256]).astype(BF)
        for z in range(4):
            nat_ref[z, :, i * 256 : (i + 1) * 256] = n4[z * 32 : (z + 1) * 32]

    for c in hid_copies:
        c.wait()
    for c in ag_copies:
        c.wait_send()
    for c in fw_copies:
        c.wait_send()

    @pl.when(row > 0)
    def _():
        low.wait_send()

    @pl.when(row < last)
    def _():
        high.wait_send()

    own.wait()
    for c in back_copies:
        c.wait()


def fine_kernel(child_ref, x_ref, hid_ref, back_ref, wd_ref, ws_ref, out_ref, up, lifted):
    step = pl.program_id(0)

    @pl.when(step == 0)
    def _():
        where = column_of(iota((256, 512), 1))
        line = iota((256, 512), 0)
        for k in range(4):
            up[k] = jnp.where(line == where + 64 * k, 1.0, 0.0).astype(BF)
        for w in range(8):
            r = jnp.concatenate([back_ref[j, w * 32 : (w + 1) * 32, :] for j in range(8)], axis=0)
            lifted[w * 128 : (w + 1) * 128, :] = tn(r, wd_ref[...])

    skips = []
    for g in range(TB // 4):
        dec = []
        for k in range(4):
            s = 4 * g + k
            lift = lifted[pl.ds(step * TB + s, 8, stride=128), :]
            lift = jnp.where(child_ref[step * TB + s] >= 0, lift, -3e38)
            h = hid_ref[s * 64 : (s + 1) * 64, :].astype(F32).reshape(8, 8, 128)
            dec.append(jnp.maximum(h + lift[None], 0.0).reshape(64, 128).astype(BF))
        skips.append(nt(ws_ref[...], jnp.concatenate(dec, axis=0)).astype(BF))
    skip = jnp.concatenate(skips, axis=0)
    for k in range(4):
        r = mm(skip, up[k])
        for g in range(TB // 4):
            s = 4 * g + k
            out_ref[s] = (x_ref[s].astype(F32) + r[g * 64 : (g + 1) * 64]).astype(BF)


def shards(
    fine_feats, fine_child, parent_block, w_parent, w_root_in, w_root, root_bias, w_down, w_skip
):
    rows = lax.axis_size("row")
    wc = w_root.transpose(2, 3, 4, 0, 1).reshape(864, 256)
    vm = pl.BlockSpec(memory_space=pltpu.VMEM)
    anym = pl.BlockSpec(memory_space=pl.ANY)
    dma = pltpu.SemaphoreType.DMA
    hidden, back, nat = pl.pallas_call(
        functools.partial(root_kernel, rows),
        name="root",
        out_shape=(
            jax.ShapeDtypeStruct((SLOTS * 64, 128), BF),
            jax.ShapeDtypeStruct((8, 256, 128), BF),
            jax.ShapeDtypeStruct((4, 32, 1024), BF),
        ),
        in_specs=[vm, vm, anym, vm, vm, vm, vm],
        out_specs=(anym, anym, vm),
        scratch_shapes=[
            pltpu.VMEM((NB, SB, 64, 512), BF),
            pltpu.VMEM((4, 512, 256), BF),
            pltpu.VMEM((NB * SB * 64, 128), BF),
            pltpu.VMEM((SB * 8, 128), F32),
            pltpu.VMEM((8, 8, 128), I32),
            pltpu.VMEM((1024, 1024), BF),
            pltpu.VMEM((512, 1024), BF),
            pltpu.VMEM((512, 1024), BF),
            pltpu.VMEM((2, 256, 512), BF),
            pltpu.VMEM((6, 4, 256, 256), BF),
            pltpu.VMEM((4, 288, 256), F32),
            pltpu.VMEM((256, 512), BF),
            pltpu.VMEM((128, 1024), BF),
            pltpu.VMEM((1024, 1024), BF),
            pltpu.VMEM((8, 256, 128), BF),
            dma((NB,)),
            dma((NB,)),
            dma((8,)),
            dma((8,)),
            dma((NB, 4)),
            dma((NB, 4)),
            dma((NB, 4)),
            dma((NB, 4)),
            dma((2,)),
            dma((2,)),
            dma((8,)),
            dma((8,)),
            dma,
        ],
        compiler_params=pltpu.CompilerParams(
            collective_id=0, has_side_effects=True, vmem_limit_bytes=60 * 1024 * 1024
        ),
    )(
        fine_child.reshape(1, SLOTS),
        parent_block.reshape(1, 8),
        fine_feats,
        w_parent,
        w_root_in,
        wc,
        root_bias.reshape(1, 32),
    )
    full = lambda shape: pl.BlockSpec(shape, lambda i: (0,) * len(shape))
    fine_out = pl.pallas_call(
        fine_kernel,
        name="fine",
        grid=(SLOTS // TB,),
        out_shape=jax.ShapeDtypeStruct((SLOTS, 64, 512), BF),
        in_specs=[
            pl.BlockSpec(memory_space=pltpu.SMEM),
            pl.BlockSpec((TB, 64, 512), lambda i: (i, 0, 0)),
            pl.BlockSpec((TB * 64, 128), lambda i: (i, 0)),
            full((8, 256, 128)),
            full((256, 128)),
            full((64, 128)),
        ],
        out_specs=pl.BlockSpec((TB, 64, 512), lambda i: (i, 0, 0)),
        scratch_shapes=[pltpu.VMEM((4, 256, 512), BF), pltpu.VMEM((1024, 128), F32)],
        compiler_params=pltpu.CompilerParams(vmem_limit_bytes=48 * 1024 * 1024),
    )(fine_child, fine_feats, hidden, back, w_down, w_skip.T)
    root_local = nat.transpose(1, 0, 2).reshape(32, 4, 32, 32)
    return (fine_out, root_local)


def solution(mesh):
    return jax.shard_map(
        shards,
        mesh=mesh,
        in_specs=(
            P(("row", "ga"), None, None),
            P(("row", "ga")),
            P(("row", "ga")),
            P(),
            P(),
            P("ga", None, None, None, None),
            P("ga"),
            P(),
            P(),
        ),
        out_specs=(P(("row", "ga"), None, None), P("ga", "row", None, None)),
        check_vma=False,
    )
```

profile of v0, /device:TPU:96, one launch (start us, length us, event | category | flops | bytes accessed | tf_op | source)
XLA Modules:
  0.0 57.9 jit_solution(7819276497582437941)
XLA Ops:
  0.6 0.0 copy-start.4
  0.6 0.0 copy-start.3
  0.7 0.0 copy-start.2
  0.7 42.1 %root.1 = (bf16[7680,128]{1,0:T(8,128)(2,1)}, bf16[8,256,128]{2,1,0:T(8,128)(2,1)}, bf16[4,32,1024]{2,1,0:T(8,128)(2,1)}) custom-call(s32[1,120]{1,0:T(1,128)} %bitcast.11, s32[1,8]{1,0:T(1,128)} %bitcast.14, bf16[120,64,512]{2,1,0:T(8,128)(2,1)} %x_ref.1, bf16[64,128]{1,0:T(8,128)(2,1)} %wp_ref.1, bf16[128,256]{1,0:T(8,128)(2,1)} %win_ref.1, ...), custom_call_target="tpu_custom_call" | custom-call | tf_op jit(solution)/shard_map/root/pallas_call | solution.py:449
  42.8 0.0 copy-done.4
  42.8 0.0 copy-done.3
  42.8 0.0 copy-done.2
  42.8 0.0 copy-start
  42.8 1.5 %copy-done = bf16[7680,128]{1,0:T(8,128)(2,1)S(1)} copy-done((bf16[7680,128]{1,0:T(8,128)(2,1)S(1)}, bf16[7680,128]{1,0:T(8,128)(2,1)}, u32[]{:S(2)}) %copy-start) | copy-done | bytes 1966104
  44.3 0.0 copy-start.1
  44.3 1.0 %copy-done.1 = bf16[8,256,128]{2,1,0:T(8,128)(2,1)S(1)} copy-done((bf16[8,256,128]{2,1,0:T(8,128)(2,1)S(1)}, bf16[8,256,128]{2,1,0:T(8,128)(2,1)}, u32[]{:S(2)}) %copy-start.1) | copy-done | bytes 524312
  45.4 0.0 copy-start.5
  45.4 10.6 %fine.1 = bf16[120,64,512]{2,1,0:T(8,128)(2,1)} custom-call(s32[120]{0:T(128)S(1)} %copy-done.4, bf16[120,64,512]{2,1,0:T(8,128)(2,1)} %x_ref.1, bf16[7680,128]{1,0:T(8,128)(2,1)S(1)} %copy-done, bf16[8,256,128]{2,1,0:T(8,128)(2,1)S(1)} %copy-done.1, bf16[256,128]{1,0:T(8,128)(2,1)S(1)} %copy-done.2, bf16[64,128]{1,0:T(8,128)(2,1)S(1)} %bitcast.10), custom_call_target="tpu_custom_call" | custom-call | tf_op jit(solution)/shard_map/fine/pallas_call | solution.py:502
  56.0 0.0 copy-done.5
  56.0 0.8 %reshape.23 = bf16[32,4,32,32]{3,2,0,1:T(8,128)(2,1)S(1)} reshape(bf16[32,4,1024]{2,0,1:T(8,128)(2,1)S(1)} %bitcast.13) | data formatting | bytes 524288 | tf_op jit(solution)/shard_map/reshape | solution.py:519
  56.8 1.1 %copy.11 = bf16[32,4,32,32]{3,2,1,0:T(8,128)(2,1)} copy(bf16[32,4,32,32]{3,2,0,1:T(8,128)(2,1)S(1)} %reshape.23) | data formatting | bytes 524288
Async XLA Ops:
  0.6 42.1 %copy-start.4 = (s32[120]{0:T(128)S(1)}, s32[120]{0:T(128)}, u32[]{:S(2)}) copy-start(s32[120]{0:T(128)} %child_ref.1) | copy-start | bytes 1444
  0.6 42.1 %copy-start.3 = (bf16[128,64]{0,1:T(8,128)(2,1)S(1)}, bf16[128,64]{0,1:T(8,128)(2,1)}, u32[]{:S(2)}) copy-start(bf16[128,64]{0,1:T(8,128)(2,1)} %param.17) | copy-start | bytes 49156
  0.7 42.1 %copy-start.2 = (bf16[256,128]{1,0:T(8,128)(2,1)S(1)}, bf16[256,128]{1,0:T(8,128)(2,1)}, u32[]{:S(2)}) copy-start(bf16[256,128]{1,0:T(8,128)(2,1)} %wd_ref.1) | copy-start | bytes 196612
  42.8 1.5 %copy-start = (bf16[7680,128]{1,0:T(8,128)(2,1)S(1)}, bf16[7680,128]{1,0:T(8,128)(2,1)}, u32[]{:S(2)}) copy-start(bf16[7680,128]{1,0:T(8,128)(2,1)} %get-tuple-element.5.hid_ref) | copy-start | bytes 5898244
  44.3 1.0 %copy-start.1 = (bf16[8,256,128]{2,1,0:T(8,128)(2,1)S(1)}, bf16[8,256,128]{2,1,0:T(8,128)(2,1)}, u32[]{:S(2)}) copy-start(bf16[8,256,128]{2,1,0:T(8,128)(2,1)} %get-tuple-element.6.back_ref) | copy-start | bytes 1572868
  45.4 10.6 %copy-start.5 = (bf16[4,32,1024]{2,1,0:T(8,128)(2,1)S(1)}, bf16[4,32,1024]{2,1,0:T(8,128)(2,1)}, u32[]{:S(2)}) copy-start(bf16[4,32,1024]{2,1,0:T(8,128)(2,1)} %get-tuple-element.7) | copy-start | bytes 786436
where the time goes:
time: 58.2 us; the launch traced here: 57.9 us
  Pallas kernels  52.7 us (91%)
  local copies, waits for them, and re-layouts  4.48 us (8%)
  between operations  0.71 us (1%)
    pallas_call x1, Pallas kernels, shards(): pl.pallas_call(functools.partial(root_kernel, rows), name='root', out_sha...  42.1 us
    pallas_call x1, Pallas kernels, shards(): pl.pallas_call(fine_kernel, name='fine', grid=(SLOTS // TB,), out_shape=j...  10.6 us
    unnamed x13, local copies, waits for them, and re-layouts  3.71 us

commit v1 on v0

v1 whole, which is shorter than its diff:
```python
import functools

import jax
import jax.numpy as jnp
from jax import lax
from jax.experimental import pallas as pl
from jax.experimental.pallas import tpu as pltpu
from jax.sharding import PartitionSpec as P

BF = jnp.bfloat16
F32 = jnp.float32
I32 = jnp.int32
MESH = pl.DeviceIdType.MESH
SLOTS = 120
NB = 4
SB = 32
TB = 24
OUT = jax.ShapeDtypeStruct
ROOT_MB = 40
FINE_MB = 24


def in_hbm(a):
    return pltpu.with_memory_space_constraint(a, pltpu.HBM)


def iota(shape, dim):
    return lax.broadcasted_iota(I32, shape, dim)


def column_of(v):
    z, y, x = v >> 6, (v >> 3) & 7, v & 7
    w = (z >> 2) * 4 + (y >> 2) * 2 + (x >> 2)
    g = ((z >> 1) & 1) * 4 + ((y >> 1) & 1) * 2 + ((x >> 1) & 1)
    return g * 8 + w


def nt(a, b):
    return lax.dot_general(a, b, (((1,), (1,)), ((), ())), preferred_element_type=F32)


def tn(a, b):
    return lax.dot_general(a, b, (((0,), (0,)), ((), ())), preferred_element_type=F32)


def mm(a, b):
    return jnp.dot(a, b, preferred_element_type=F32)


def root_kernel(
    rows,
    child_hbm,
    block_hbm,
    x_hbm,
    wp_hbm,
    win_hbm,
    wc_hbm,
    bias_hbm,
    x_ref,
    hid_ref,
    back_ref,
    feat_ref,
    child_ref,
    block_ref,
    wp_ref,
    win_ref,
    wc_ref,
    bias_ref,
    p8,
    pp,
    ints,
    gathered,
    place,
    slab,
    halo,
    weff,
    taps,
    rft,
    quad,
    perm,
    flat,
    msgs,
    x_sem,
    w_sem,
    int_send,
    int_recv,
    ag_send,
    ag_recv,
    fw_send,
    fw_recv,
    halo_send,
    halo_recv,
    back_send,
    back_recv,
    own_sem,
):
    row = lax.axis_index("row")
    me = lax.axis_index("ga")
    chip = me // 2
    core = lax.rem(me, 2)
    partner = 2 * chip + 1 - core
    last = rows - 1

    def peer(k):
        return lax.rem(me + k, 8)

    def chip_peer(k):
        return 2 * lax.rem(chip + k, 4) + core

    def remote(src, dst, send, recv, row_at, ga):
        return pltpu.make_async_remote_copy(
            src, dst, send, recv, device_id=(row_at, ga), device_id_type=MESH
        )

    x_copies = []
    for blk in range(NB):
        n = min(SB, SLOTS - blk * SB)
        part = pl.ds(blk * SB, n)
        x_copies.append(pltpu.make_async_copy(x_hbm.at[part], x_ref.at[part], x_sem.at[blk]))
        x_copies[-1].start()

    pairs = [
        (child_hbm, child_ref),
        (block_hbm, block_ref),
        (wp_hbm, wp_ref),
        (win_hbm, win_ref),
        (wc_hbm, wc_ref),
        (bias_hbm, bias_ref),
    ]
    small = [pltpu.make_async_copy(p, q, w_sem.at[i]) for i, (p, q) in enumerate(pairs)]
    for c in small:
        c.start()

    barrier = pltpu.get_barrier_semaphore()
    for k in range(1, 8):
        pl.semaphore_signal(barrier, inc=1, device_id=(row, peer(k)), device_id_type=MESH)

    @pl.when(row > 0)
    def _():
        pl.semaphore_signal(barrier, inc=1, device_id=(row - 1, me), device_id_type=MESH)

    @pl.when(row < last)
    def _():
        pl.semaphore_signal(barrier, inc=1, device_id=(row + 1, me), device_id_type=MESH)

    where = column_of(iota((512, 256), 0))
    lane = iota((512, 256), 1)
    for k in range(4):
        p8[k * 512 : (k + 1) * 512] = jnp.where(lane == where + 64 * k, 0.125, 0.0).astype(BF)
    small[0].wait()
    small[1].wait()
    ints[me] = jnp.full((8, 128), -1, I32)
    ints[me, 0:1, 0:SLOTS] = child_ref[...]
    ints[me, 1:2, 0:8] = block_ref[...]
    small[2].wait()

    int_copies, ag_sent, fw_copies = [], [], []

    def piece(ga, blk):
        return gathered.at[pl.ds(pl.multiple_of(ga * 128 + blk * SB, SB), SB)]

    def forward(ga, blk, k):
        c = remote(
            piece(ga, blk), piece(ga, blk), fw_send.at[blk, k], fw_recv.at[blk, k], row, partner
        )
        c.start()
        fw_copies.append(c)

    def send(ga, blk, k, to):
        c = remote(
            piece(ga, blk), piece(ga, blk), ag_send.at[blk, k], ag_recv.at[blk, k], row, to
        )
        c.start()
        ag_sent.append(c)

    def arrived(ga, blk, k):
        remote(
            piece(me, blk), piece(ga, blk), ag_send.at[blk, k], ag_recv.at[blk, k], row, partner
        ).wait_recv()

    right, left, far = chip_peer(1), chip_peer(3), chip_peer(2)

    def relay(blk):
        first, onward = (0, right) if blk % 2 == 0 else (1, left)
        for k in (first, 1 - first):
            src = left if k == 0 else right
            arrived(src, blk, k)
            if k == first:
                send(src, blk, 2, onward)
            forward(src, blk, 1 + k)

    def far_block(blk):
        arrived(far, blk, 2)
        forward(far, blk, 3)

    for blk in range(NB):
        x_copies[blk].wait()
        n = min(SB, SLOTS - blk * SB)
        x = jnp.concatenate(
            [
                jnp.concatenate([x_ref[blk * SB + 4 * g + k] for k in range(4)], axis=1)
                for g in range(n // 4)
            ],
            axis=0,
        )
        pooled = mm(x, p8[...]).astype(BF)
        for g in range(n // 4):
            h = tn(pooled[g * 64 : (g + 1) * 64], wp_ref[...])
            h = jnp.maximum(h, 0.0).astype(BF)
            hid_ref[pl.ds((blk * SB + 4 * g) * 64, 256), :] = h
            mean = jnp.sum(h.astype(F32).reshape(4, 8, 8, 128), axis=1) * 0.125
            pp[pl.ds(g * 32, 32), :] = mean.reshape(32, 128)
        if n < SB:
            pp[pl.ds(n * 8, (SB - n) * 8), :] = jnp.zeros(((SB - n) * 8, 128), F32)
        start = pl.multiple_of(me * 128 + blk * SB, SB)
        for w in range(8):
            gathered[pl.ds(start, SB), w * 128 : (w + 1) * 128] = pp[
                pl.ds(w, SB, stride=8), :
            ].astype(BF)
        if blk == 0:
            sides = (row > 0).astype(I32) + (row < last).astype(I32)
            pl.semaphore_wait(barrier, 7 + sides)
        send(me, blk, 0, right)
        send(me, blk, 1, left)
        forward(me, blk, 0)
        if blk == 0:
            for k in range(1, 8):
                c = remote(ints.at[me], ints.at[me], int_send.at[k], int_recv.at[k], row, peer(k))
                c.start()
                int_copies.append(c)
        else:
            relay(blk - 1)
        if blk >= 2:
            far_block(blk - 2)

    for c in small[3:]:
        c.wait()
    weff[...] = nt(wc_ref[...], win_ref[...]).astype(BF)

    for c in int_copies:
        c.wait()
    child = jnp.concatenate([ints[m, 0:1, :] for m in range(8)], axis=0)
    parent = child >> 3
    block = jnp.zeros((8, 128), I32)
    for m in range(8):
        blocks = ints[m, 1:2, :]
        for i in range(8):
            block = jnp.where(parent == 8 * m + i, blocks[:, i : i + 1], block)
    octant = child & 7
    pos = (
        (octant >> 2) * 256
        + (2 * (block >> 3) + ((octant >> 1) & 1)) * 16
        + 2 * (block & 7)
        + (octant & 1)
    )
    pos = jnp.where(child >= 0, pos, -1)

    relay(NB - 1)
    far_block(NB - 2)
    for m in range(8):
        hot = iota((512, 128), 0) == pos[m : m + 1, :]
        place[:, m * 128 : (m + 1) * 128] = jnp.where(hot, 1.0, 0.0).astype(BF)
    far_block(NB - 1)
    for c in fw_copies:
        c.wait_recv()

    def put(half, i):
        r = pl.ds(half * 256, 256)
        c = slice(i * 256, (i + 1) * 256)
        slab[r, c] = mm(place[r, :], gathered[:, c]).astype(BF)

    low = remote(
        slab.at[pl.ds(0, 256), pl.ds(0, 512)],
        halo.at[1],
        halo_send.at[0],
        halo_recv.at[1],
        jnp.maximum(row - 1, 0),
        me,
    )
    high = remote(
        slab.at[pl.ds(256, 256), pl.ds(512, 512)],
        halo.at[0],
        halo_send.at[1],
        halo_recv.at[0],
        jnp.minimum(row + 1, last),
        me,
    )
    put(0, 0)
    put(0, 1)

    @pl.when(row > 0)
    def _():
        low.start()

    put(1, 2)
    put(1, 3)

    @pl.when(row < last)
    def _():
        high.start()

    put(0, 2)
    put(0, 3)
    put(1, 0)
    put(1, 1)

    spot = iota((32, 256), 1)
    oy, ox = spot >> 4, spot & 15
    bias = jnp.sum(
        jnp.where(iota((32, 32), 0) == iota((32, 32), 1), bias_ref[...], 0.0),
        axis=1,
        keepdims=True,
    )

    def plane(zz, ab):
        c = ((zz & 1) * 4 + ab) * 128
        return slab[pl.ds((zz >> 1) * 256, 256), c : c + 128]

    def weights(lo, hi):
        return jnp.concatenate([weff[d * 288 : (d + 1) * 288] for d in range(lo, hi)], axis=1)

    def matmuls(z):
        lo, hi = max(0, 1 - z), min(3, 5 - z)
        for ab in range(4):
            x = jnp.concatenate([plane(z - 1 + d, ab) for d in range(lo, hi)], axis=1)
            taps[z, ab] = nt(weights(lo, hi), x)

    def outer(z, side):
        d = 0 if side == 0 else 2
        for ab in range(4):
            x = halo[side, :, ab * 128 : (ab + 1) * 128]
            taps[z, ab] += nt(weights(d, d + 1), x)

    def combine(z):
        def tap(a, b, dy, dx):
            t = ((dy + 1) * 3 + dx + 1) * 32
            return taps[z, 2 * a + b, t : t + 32, :]

        for iy in range(2):
            for ix in range(2):
                ys = [(iy, 0), (1 - iy, 1 - 2 * iy)]
                xs = [(ix, 0), (1 - ix, 1 - 2 * ix)]
                ysh = (1 - iy, 2 * iy - 1)
                xsh = (1 - ix, 2 * ix - 1)
                plain = sum(tap(a, b, dy, dx) for a, dy in ys for b, dx in xs)
                only_x = sum(tap(a, xsh[0], dy, xsh[1]) for a, dy in ys)
                only_y = sum(tap(ysh[0], b, ysh[1], dx) for b, dx in xs)
                both = tap(ysh[0], xsh[0], ysh[1], xsh[1])

                def shift_x(v):
                    v = pltpu.roll(v, 255 if ix else 1, 1)
                    return jnp.where(ox == (15 if ix else 0), 0.0, v)

                def shift_y(v):
                    v = pltpu.roll(v, 240 if iy else 16, 1)
                    return jnp.where(oy == (15 if iy else 0), 0.0, v)

                total = plain + shift_x(only_x) + shift_y(only_y + shift_x(both))
                out = jnp.maximum(total + bias, 0.0).astype(BF)
                w = (z & 1) * 4 + iy * 2 + ix
                rft[w * 32 : (w + 1) * 32, (z >> 1) * 256 : ((z >> 1) + 1) * 256] = out
                r = iy * 128 + z * 32
                quad[r : r + 32, ix * 256 : (ix + 1) * 256] = out

    matmuls(1)
    matmuls(2)
    combine(1)
    combine(2)
    matmuls(0)
    matmuls(3)
    p, q = iota((512, 512), 0), iota((512, 512), 1)
    hot = q == ((p >> 4) & 15) * 32 + 2 * (p & 15) + (p >> 8)
    perm[...] = jnp.where(hot, 1.0, 0.0).astype(BF)

    @pl.when(row > 0)
    def _():
        high.wait_recv()

    @pl.when(row < last)
    def _():
        low.wait_recv()

    @pl.when(row == 0)
    def _():
        halo[0] = jnp.zeros((256, 512), BF)

    @pl.when(row == last)
    def _():
        halo[1] = jnp.zeros((256, 512), BF)

    outer(0, 0)
    outer(3, 1)
    combine(0)
    combine(3)

    for i in range(4):
        m2 = mm(rft[...], place[:, i * 256 : (i + 1) * 256]).astype(BF)
        msgs[2 * i] = m2[:, :128]
        msgs[2 * i + 1] = m2[:, 128:]
    back_copies = []
    for k in (4, 3, 5, 2, 6, 1, 7):
        c = remote(
            msgs.at[peer(k)], back_ref.at[me], back_send.at[k], back_recv.at[k], row, peer(k)
        )
        c.start()
        back_copies.append(c)
    own = pltpu.make_async_copy(msgs.at[me], back_ref.at[me], own_sem)
    own.start()

    nat = mm(quad[...], perm[...])
    for iy in range(2):
        for z in range(4):
            v = nat[iy * 128 + z * 32 : iy * 128 + z * 32 + 32]
            for t in range(16):
                tile = v[:, t // 4 * 128 : t // 4 * 128 + 128]
                if t % 4:
                    tile = pltpu.roll(tile, 128 - 32 * (t % 4), 1)
                flat[pl.ds(z * 32 + 2 * t + iy, 32, stride=128), :] = tile
    for c in range(32):
        f = flat[c * 128 : (c + 1) * 128, :][:, :32].astype(BF)
        feat_ref[c] = f.reshape(4, 32, 32)

    for c in ag_sent:
        c.wait_send()
    for c in fw_copies:
        c.wait_send()

    @pl.when(row > 0)
    def _():
        low.wait_send()

    @pl.when(row < last)
    def _():
        high.wait_send()

    own.wait()
    for c in back_copies:
        c.wait()


def fine_kernel(
    child_ref, x_ref, hid_ref, back_ref, wd_ref, ws_ref, feat_ref, out_ref, root_ref, up, lifted, sem
):
    step = pl.program_id(0)
    copy = pltpu.make_async_copy(feat_ref, root_ref, sem)

    @pl.when(step == 0)
    def _():
        copy.start()
        where = column_of(iota((256, 512), 1))
        line = iota((256, 512), 0)
        for k in range(4):
            up[k] = jnp.where(line == where + 64 * k, 1.0, 0.0).astype(BF)
        for w in range(8):
            r = jnp.concatenate([back_ref[j, w * 32 : (w + 1) * 32, :] for j in range(8)], axis=0)
            lifted[w * 128 : (w + 1) * 128, :] = tn(r, wd_ref[...])

    skips = []
    for g in range(TB // 4):
        dec = []
        for k in range(4):
            s = step * TB + 4 * g + k
            lift = lifted[pl.ds(s, 8, stride=128), :]
            lift = jnp.where(child_ref[s] >= 0, lift, -3e38)
            h = hid_ref[pl.ds(pl.multiple_of(s * 64, 64), 64), :].astype(F32).reshape(8, 8, 128)
            dec.append(jnp.maximum(h + lift[None], 0.0).reshape(64, 128).astype(BF))
        skips.append(nt(ws_ref[...], jnp.concatenate(dec, axis=0)).astype(BF))
    skip = jnp.concatenate(skips, axis=0)
    for k in range(4):
        r = mm(skip, up[k])
        for g in range(TB // 4):
            s = 4 * g + k
            x = x_ref[step * TB + s].astype(F32)
            out_ref[s] = (x + r[g * 64 : (g + 1) * 64]).astype(BF)

    @pl.when(step == SLOTS // TB - 1)
    def _():
        copy.wait()


def shards(
    fine_feats, fine_child, parent_block, w_parent, w_root_in, w_root, root_bias, w_down, w_skip
):
    rows = lax.axis_size("row")
    wc = w_root.transpose(2, 3, 4, 0, 1).reshape(864, 256)
    vm = pl.BlockSpec(memory_space=pltpu.VMEM)
    anym = pl.BlockSpec(memory_space=pl.ANY)
    hbm = pl.BlockSpec(memory_space=pltpu.HBM)
    dma = pltpu.SemaphoreType.DMA
    x, hidden, back, feat = pl.pallas_call(
        functools.partial(root_kernel, rows),
        name="root",
        out_shape=(
            OUT((SLOTS, 64, 512), BF),
            OUT((SLOTS * 64, 128), BF),
            OUT((8, 256, 128), BF),
            OUT((32, 4, 32, 32), BF),
        ),
        in_specs=[hbm] * 7,
        out_specs=(vm, vm, vm, vm),
        scratch_shapes=[
            pltpu.VMEM((1, SLOTS), I32),
            pltpu.VMEM((1, 8), I32),
            pltpu.VMEM((64, 128), BF),
            pltpu.VMEM((128, 256), BF),
            pltpu.VMEM((864, 256), BF),
            pltpu.VMEM((1, 32), F32),
            pltpu.VMEM((2048, 256), BF),
            pltpu.VMEM((SB * 8, 128), F32),
            pltpu.VMEM((8, 8, 128), I32),
            pltpu.VMEM((1024, 1024), BF),
            pltpu.VMEM((512, 1024), BF),
            pltpu.VMEM((512, 1024), BF),
            pltpu.VMEM((2, 256, 512), BF),
            pltpu.VMEM((864, 128), BF),
            pltpu.VMEM((4, 4, 288, 256), F32),
            pltpu.VMEM((256, 512), BF),
            pltpu.VMEM((256, 512), BF),
            pltpu.VMEM((512, 512), BF),
            pltpu.VMEM((4096, 128), F32),
            pltpu.VMEM((8, 256, 128), BF),
            dma((NB,)),
            dma((6,)),
            dma((8,)),
            dma((8,)),
            dma((NB, 3)),
            dma((NB, 3)),
            dma((NB, 4)),
            dma((NB, 4)),
            dma((2,)),
            dma((2,)),
            dma((8,)),
            dma((8,)),
            dma,
        ],
        compiler_params=pltpu.CompilerParams(
            collective_id=0, has_side_effects=True, vmem_limit_bytes=ROOT_MB * 1024 * 1024
        ),
    )(
        in_hbm(fine_child.reshape(1, SLOTS)),
        in_hbm(parent_block.reshape(1, 8)),
        in_hbm(fine_feats),
        in_hbm(w_parent),
        in_hbm(w_root_in),
        in_hbm(wc),
        in_hbm(root_bias.reshape(1, 32)),
    )
    return pl.pallas_call(
        fine_kernel,
        name="fine",
        grid=(SLOTS // TB,),
        out_shape=(
            jax.ShapeDtypeStruct((SLOTS, 64, 512), BF),
            jax.ShapeDtypeStruct((32, 4, 32, 32), BF),
        ),
        in_specs=[pl.BlockSpec(memory_space=pltpu.SMEM), vm, vm, vm, vm, vm, anym],
        out_specs=(pl.BlockSpec((TB, 64, 512), lambda i: (i, 0, 0)), anym),
        scratch_shapes=[
            pltpu.VMEM((4, 256, 512), BF),
            pltpu.VMEM((1024, 128), F32),
            pltpu.SemaphoreType.DMA,
        ],
        compiler_params=pltpu.CompilerParams(vmem_limit_bytes=FINE_MB * 1024 * 1024),
    )(fine_child, x, hidden, back, w_down, w_skip.T, feat)


def solution(mesh):
    return jax.shard_map(
        shards,
        mesh=mesh,
        in_specs=(
            P(("row", "ga"), None, None),
            P(("row", "ga")),
            P(("row", "ga")),
            P(),
            P(),
            P("ga", None, None, None, None),
            P("ga"),
            P(),
            P(),
        ),
        out_specs=(P(("row", "ga"), None, None), P("ga", "row", None, None)),
        check_vma=False,
    )
```

time: 58.2 us -> 49.8 us (0.86)
  local copies, waits for them, and re-layouts: 4.48 us -> 0.01 us
  Pallas kernels: 52.7 us -> 49 us
    pallas_call x1, Pallas kernels: 10.6 us -> 6.89 us  [shards(): pl.pallas_call(fine_kernel, name='fine', grid=(SLOTS // TB,), out_shape=(...]
    unnamed x13 -> x6, local copies, waits for them, and re-layouts: 3.71 us -> 0.01 us
    reshape x1 -> x0, local copies, waits for them, and re-layouts: 0.77 us -> none  [shards(): root_local = nat.transpose(1, 0, 2).reshape(32, 4, 32, 32)]
where the time goes in v1:
time: 49.8 us; the launch traced here: 49.7 us
  Pallas kernels  49 us (98%)
  between operations  0.69 us (1%)
    pallas_call x1, Pallas kernels, shards(): pl.pallas_call(functools.partial(root_kernel, rows), name='root', out_sha...  42.1 us
    pallas_call x1, Pallas kernels, shards(): pl.pallas_call(fine_kernel, name='fine', grid=(SLOTS // TB,), out_shape=(...  6.89 us

profile of v1, /device:TPU:96, one launch (start us, length us, event | category | flops | bytes accessed | tf_op | source)
XLA Modules:
  0.0 49.7 jit_solution(2672625289834888497)
XLA Ops:
  0.6 0.0 copy-start.2
  0.6 0.0 copy-start.1
  0.7 0.0 copy-start
  0.7 42.1 %root.1 = (bf16[120,64,512]{2,1,0:T(8,128)(2,1)S(1)}, bf16[7680,128]{1,0:T(8,128)(2,1)S(1)}, bf16[8,256,128]{2,1,0:T(8,128)(2,1)S(1)}, bf16[32,4,32,32]{3,2,1,0:T(8,128)(2,1)S(1)}) custom-call(s32[1,120]{1,0:T(1,128)} %bitcast.8, s32[1,8]{1,0:T(1,128)} %bitcast.10, bf16[120,64,512]{2,1,0:T(8,128)(2,1)} %x_hbm.1, bf16[64,128]{1,0:T(8,128)(2,1)} %wp_hbm.1, ...), custom_call_target="tpu_custom_call" | custom-call | tf_op jit(solution)/shard_map/root/pallas_call | solution.py:490
  42.8 0.0 copy-done.2
  42.8 0.0 copy-done.1
  42.8 0.0 copy-done
  42.8 6.9 %fine.1 = (bf16[120,64,512]{2,1,0:T(8,128)(2,1)}, bf16[32,4,32,32]{3,2,1,0:T(8,128)(2,1)}) custom-call(s32[120]{0:T(128)S(1)} %copy-done.2, bf16[120,64,512]{2,1,0:T(8,128)(2,1)S(1)} %get-tuple-element.6.x_ref, bf16[7680,128]{1,0:T(8,128)(2,1)S(1)} %get-tuple-element.7.hid_ref, bf16[8,256,128]{2,1,0:T(8,128)(2,1)S(1)} %get-tuple-element.8.back_ref, ...), custom_call_target="tpu_custom_call" | custom-call | tf_op jit(solution)/shard_map/fine/pallas_call | solution.py:548
Async XLA Ops:
  0.6 42.1 %copy-start.2 = (s32[120]{0:T(128)S(1)}, s32[120]{0:T(128)}, u32[]{:S(2)}) copy-start(s32[120]{0:T(128)} %child_ref.1) | copy-start | bytes 1444
  0.6 42.1 %copy-start.1 = (bf16[128,64]{0,1:T(8,128)(2,1)S(1)}, bf16[128,64]{0,1:T(8,128)(2,1)}, u32[]{:S(2)}) copy-start(bf16[128,64]{0,1:T(8,128)(2,1)} %param.17) | copy-start | bytes 49156
  0.7 42.1 %copy-start = (bf16[256,128]{1,0:T(8,128)(2,1)S(1)}, bf16[256,128]{1,0:T(8,128)(2,1)}, u32[]{:S(2)}) copy-start(bf16[256,128]{1,0:T(8,128)(2,1)} %wd_ref.1) | copy-start | bytes 196612

commit v2 on v1

--- a/solution.py
+++ b/solution.py
@@ -12,8 +12,8 @@
 I32 = jnp.int32
 MESH = pl.DeviceIdType.MESH
 SLOTS = 120
-NB = 4
-SB = 32
+BLOCKS = ((0, 16, 16), (16, 32, 32), (48, 32, 32), (80, 32, 32), (112, 8, 16))
+NB = len(BLOCKS)
 TB = 24
 OUT = jax.ShapeDtypeStruct
 ROOT_MB = 40
@@ -90,6 +90,8 @@
     fw_recv,
     halo_send,
     halo_recv,
+    swap_send,
+    swap_recv,
     back_send,
     back_recv,
     own_sem,
@@ -113,9 +115,8 @@
         )
 
     x_copies = []
-    for blk in range(NB):
-        n = min(SB, SLOTS - blk * SB)
-        part = pl.ds(blk * SB, n)
+    for blk, (first, n, _) in enumerate(BLOCKS):
+        part = pl.ds(first, n)
         x_copies.append(pltpu.make_async_copy(x_hbm.at[part], x_ref.at[part], x_sem.at[blk]))
         x_copies[-1].start()
 
@@ -157,7 +158,8 @@
     int_copies, ag_sent, fw_copies = [], [], []
 
     def piece(ga, blk):
-        return gathered.at[pl.ds(pl.multiple_of(ga * 128 + blk * SB, SB), SB)]
+        first, _, sent = BLOCKS[blk]
+        return gathered.at[pl.ds(pl.multiple_of(ga * 128 + first, 16), sent)]
 
     def forward(ga, blk, k):
         c = remote(
@@ -173,32 +175,24 @@
         c.start()
         ag_sent.append(c)
 
-    def arrived(ga, blk, k):
+    right, left, far = chip_peer(1), chip_peer(3), chip_peer(2)
+    relays = {1: (0, right), 2: (1, left)}
+    origin = (left, right, far)
+
+    def arrived(blk, k):
+        ga = origin[k]
         remote(
             piece(me, blk), piece(ga, blk), ag_send.at[blk, k], ag_recv.at[blk, k], row, partner
         ).wait_recv()
-
-    right, left, far = chip_peer(1), chip_peer(3), chip_peer(2)
-
-    def relay(blk):
-        first, onward = (0, right) if blk % 2 == 0 else (1, left)
-        for k in (first, 1 - first):
-            src = left if k == 0 else right
-            arrived(src, blk, k)
-            if k == first:
-                send(src, blk, 2, onward)
-            forward(src, blk, 1 + k)
-
-    def far_block(blk):
-        arrived(far, blk, 2)
-        forward(far, blk, 3)
-
-    for blk in range(NB):
+        if blk in relays and relays[blk][0] == k:
+            send(ga, blk, 2, relays[blk][1])
+        forward(ga, blk, 1 + k)
+
+    for blk, (first, n, sent) in enumerate(BLOCKS):
         x_copies[blk].wait()
-        n = min(SB, SLOTS - blk * SB)
         x = jnp.concatenate(
             [
-                jnp.concatenate([x_ref[blk * SB + 4 * g + k] for k in range(4)], axis=1)
+                jnp.concatenate([x_ref[first + 4 * g + k] for k in range(4)], axis=1)
                 for g in range(n // 4)
             ],
             axis=0,
@@ -207,19 +201,21 @@
         for g in range(n // 4):
             h = tn(pooled[g * 64 : (g + 1) * 64], wp_ref[...])
             h = jnp.maximum(h, 0.0).astype(BF)
-            hid_ref[pl.ds((blk * SB + 4 * g) * 64, 256), :] = h
+            hid_ref[pl.ds((first + 4 * g) * 64, 256), :] = h
             mean = jnp.sum(h.astype(F32).reshape(4, 8, 8, 128), axis=1) * 0.125
             pp[pl.ds(g * 32, 32), :] = mean.reshape(32, 128)
-        if n < SB:
-            pp[pl.ds(n * 8, (SB - n) * 8), :] = jnp.zeros(((SB - n) * 8, 128), F32)
-        start = pl.multiple_of(me * 128 + blk * SB, SB)
+        if n < sent:
+            pp[pl.ds(n * 8, (sent - n) * 8), :] = jnp.zeros(((sent - n) * 8, 128), F32)
+        start = pl.multiple_of(me * 128 + first, 16)
         for w in range(8):
-            gathered[pl.ds(start, SB), w * 128 : (w + 1) * 128] = pp[
-                pl.ds(w, SB, stride=8), :
+            gathered[pl.ds(start, sent), w * 128 : (w + 1) * 128] = pp[
+                pl.ds(w, sent, stride=8), :
             ].astype(BF)
         if blk == 0:
             sides = (row > 0).astype(I32) + (row < last).astype(I32)
             pl.semaphore_wait(barrier, 7 + sides)
+        if blk not in relays:
+            send(me, blk, 2, far)
         send(me, blk, 0, right)
         send(me, blk, 1, left)
         forward(me, blk, 0)
@@ -228,10 +224,8 @@
                 c = remote(ints.at[me], ints.at[me], int_send.at[k], int_recv.at[k], row, peer(k))
                 c.start()
                 int_copies.append(c)
-        else:
-            relay(blk - 1)
-        if blk >= 2:
-            far_block(blk - 2)
+        if blk >= 3:
+            arrived(blk - 2, relays[blk - 2][0])
 
     for c in small[3:]:
         c.wait()
@@ -255,12 +249,13 @@
     )
     pos = jnp.where(child >= 0, pos, -1)
 
-    relay(NB - 1)
-    far_block(NB - 2)
     for m in range(8):
         hot = iota((512, 128), 0) == pos[m : m + 1, :]
         place[:, m * 128 : (m + 1) * 128] = jnp.where(hot, 1.0, 0.0).astype(BF)
-    far_block(NB - 1)
+    for blk in range(NB):
+        for k in (0, 1, 2):
+            if blk not in relays or relays[blk][0] != k:
+                arrived(blk, k)
     for c in fw_copies:
         c.wait_recv()
 
@@ -269,22 +264,34 @@
         c = slice(i * 256, (i + 1) * 256)
         slab[r, c] = mm(place[r, :], gathered[:, c]).astype(BF)
 
+    near = pl.ds(pl.multiple_of(core * 256, 256), 256)
     low = remote(
-        slab.at[pl.ds(0, 256), pl.ds(0, 512)],
-        halo.at[1],
+        slab.at[pl.ds(0, 256), near],
+        halo.at[1, core],
         halo_send.at[0],
         halo_recv.at[1],
         jnp.maximum(row - 1, 0),
         me,
     )
     high = remote(
-        slab.at[pl.ds(256, 256), pl.ds(512, 512)],
-        halo.at[0],
+        slab.at[pl.ds(256, 256), pl.ds(pl.multiple_of(512 + core * 256, 256), 256)],
+        halo.at[0, core],
         halo_send.at[1],
         halo_recv.at[0],
         jnp.minimum(row + 1, last),
         me,
     )
+    swaps = [
+        remote(
+            halo.at[side, core],
+            halo.at[side, core],
+            swap_send.at[side],
+            swap_recv.at[side],
+            row,
+            partner,
+        )
+        for side in range(2)
+    ]
     put(0, 0)
     put(0, 1)
 
@@ -325,11 +332,11 @@
             x = jnp.concatenate([plane(z - 1 + d, ab) for d in range(lo, hi)], axis=1)
             taps[z, ab] = nt(weights(lo, hi), x)
 
-    def outer(z, side):
+    def outer(z, side, half):
         d = 0 if side == 0 else 2
-        for ab in range(4):
-            x = halo[side, :, ab * 128 : (ab + 1) * 128]
-            taps[z, ab] += nt(weights(d, d + 1), x)
+        for i in range(2):
+            x = halo[side, half, :, i * 128 : (i + 1) * 128]
+            taps[z, 2 * half + i] += nt(weights(d, d + 1), x)
 
     def combine(z):
         def tap(a, b, dy, dx):
@@ -357,15 +364,47 @@
 
                 total = plain + shift_x(only_x) + shift_y(only_y + shift_x(both))
                 out = jnp.maximum(total + bias, 0.0).astype(BF)
-                w = (z & 1) * 4 + iy * 2 + ix
-                rft[w * 32 : (w + 1) * 32, (z >> 1) * 256 : ((z >> 1) + 1) * 256] = out
+                r = (iy * 2 + ix) * 32
+                part = 0 if z in (1, 2) else 1
+                rft[part, r : r + 32, (z >> 1) * 256 : ((z >> 1) + 1) * 256] = out
                 r = iy * 128 + z * 32
                 quad[r : r + 32, ix * 256 : (ix + 1) * 256] = out
+
+    back_copies, own_copies = [], []
+
+    def give_back(part):
+        for i in range(4):
+            m2 = mm(rft[part], place[:, i * 256 : (i + 1) * 256]).astype(BF)
+            msgs[part, 2 * i] = m2[:, :128]
+            msgs[part, 2 * i + 1] = m2[:, 128:]
+        for k in (4, 3, 5, 2, 6, 1, 7):
+            c = remote(
+                msgs.at[part, peer(k)],
+                back_ref.at[part, me],
+                back_send.at[part, k],
+                back_recv.at[part, k],
+                row,
+                peer(k),
+            )
+            c.start()
+            back_copies.append(c)
+        c = pltpu.make_async_copy(msgs.at[part, me], back_ref.at[part, me], own_sem.at[part])
+        c.start()
+        own_copies.append(c)
+
+    @pl.when(row == 0)
+    def _():
+        halo[0] = jnp.zeros((2, 256, 256), BF)
+
+    @pl.when(row == last)
+    def _():
+        halo[1] = jnp.zeros((2, 256, 256), BF)
 
     matmuls(1)
     matmuls(2)
     combine(1)
     combine(2)
+    give_back(0)
     matmuls(0)
     matmuls(3)
     p, q = iota((512, 512), 0), iota((512, 512), 1)
@@ -375,37 +414,29 @@
     @pl.when(row > 0)
     def _():
         high.wait_recv()
+        swaps[0].start()
 
     @pl.when(row < last)
     def _():
         low.wait_recv()
-
-    @pl.when(row == 0)
-    def _():
-        halo[0] = jnp.zeros((256, 512), BF)
-
-    @pl.when(row == last)
-    def _():
-        halo[1] = jnp.zeros((256, 512), BF)
-
-    outer(0, 0)
-    outer(3, 1)
+        swaps[1].start()
+
+    outer(0, 0, core)
+    outer(3, 1, core)
+
+    @pl.when(row > 0)
+    def _():
+        swaps[0].wait_recv()
+
+    @pl.when(row < last)
+    def _():
+        swaps[1].wait_recv()
+
+    outer(0, 0, 1 - core)
+    outer(3, 1, 1 - core)
     combine(0)
     combine(3)
-
-    for i in range(4):
-        m2 = mm(rft[...], place[:, i * 256 : (i + 1) * 256]).astype(BF)
-        msgs[2 * i] = m2[:, :128]
-        msgs[2 * i + 1] = m2[:, 128:]
-    back_copies = []
-    for k in (4, 3, 5, 2, 6, 1, 7):
-        c = remote(
-            msgs.at[peer(k)], back_ref.at[me], back_send.at[k], back_recv.at[k], row, peer(k)
-        )
-        c.start()
-        back_copies.append(c)
-    own = pltpu.make_async_copy(msgs.at[me], back_ref.at[me], own_sem)
-    own.start()
+    give_back(1)
 
     nat = mm(quad[...], perm[...])
     for iy in range(2):
@@ -428,12 +459,15 @@
     @pl.when(row > 0)
     def _():
         low.wait_send()
+        swaps[0].wait_send()
 
     @pl.when(row < last)
     def _():
         high.wait_send()
-
-    own.wait()
+        swaps[1].wait_send()
+
+    for c in own_copies:
+        c.wait()
     for c in back_copies:
         c.wait()
 
@@ -451,17 +485,20 @@
         line = iota((256, 512), 0)
         for k in range(4):
             up[k] = jnp.where(line == where + 64 * k, 1.0, 0.0).astype(BF)
-        for w in range(8):
-            r = jnp.concatenate([back_ref[j, w * 32 : (w + 1) * 32, :] for j in range(8)], axis=0)
-            lifted[w * 128 : (w + 1) * 128, :] = tn(r, wd_ref[...])
+        for i in range(8):
+            rows = slice(i % 4 * 32, i % 4 * 32 + 32)
+            r = jnp.concatenate([back_ref[i // 4, j, rows, :] for j in range(8)], axis=0)
+            lifted[i * 128 : (i + 1) * 128, :] = tn(r, wd_ref[...])
 
     skips = []
     for g in range(TB // 4):
         dec = []
         for k in range(4):
             s = step * TB + 4 * g + k
+            child = child_ref[s]
             lift = lifted[pl.ds(s, 8, stride=128), :]
-            lift = jnp.where(child_ref[s] >= 0, lift, -3e38)
+            lift = jnp.where((child >> 2) & 1 == 0, pltpu.roll(lift, 4, 0), lift)
+            lift = jnp.where(child >= 0, lift, -3e38)
             h = hid_ref[pl.ds(pl.multiple_of(s * 64, 64), 64), :].astype(F32).reshape(8, 8, 128)
             dec.append(jnp.maximum(h + lift[None], 0.0).reshape(64, 128).astype(BF))
         skips.append(nt(ws_ref[...], jnp.concatenate(dec, axis=0)).astype(BF))
@@ -493,7 +530,7 @@
         out_shape=(
             OUT((SLOTS, 64, 512), BF),
             OUT((SLOTS * 64, 128), BF),
-            OUT((8, 256, 128), BF),
+            OUT((2, 8, 128, 128), BF),
             OUT((32, 4, 32, 32), BF),
         ),
         in_specs=[hbm] * 7,
@@ -506,19 +543,19 @@
             pltpu.VMEM((864, 256), BF),
             pltpu.VMEM((1, 32), F32),
             pltpu.VMEM((2048, 256), BF),
-            pltpu.VMEM((SB * 8, 128), F32),
+            pltpu.VMEM((256, 128), F32),
             pltpu.VMEM((8, 8, 128), I32),
             pltpu.VMEM((1024, 1024), BF),
             pltpu.VMEM((512, 1024), BF),
             pltpu.VMEM((512, 1024), BF),
-            pltpu.VMEM((2, 256, 512), BF),
+            pltpu.VMEM((2, 2, 256, 256), BF),
             pltpu.VMEM((864, 128), BF),
             pltpu.VMEM((4, 4, 288, 256), F32),
-            pltpu.VMEM((256, 512), BF),
+            pltpu.VMEM((2, 128, 512), BF),
             pltpu.VMEM((256, 512), BF),
             pltpu.VMEM((512, 512), BF),
             pltpu.VMEM((4096, 128), F32),
-            pltpu.VMEM((8, 256, 128), BF),
+            pltpu.VMEM((2, 8, 128, 128), BF),
             dma((NB,)),
             dma((6,)),
             dma((8,)),
@@ -529,9 +566,11 @@
             dma((NB, 4)),
             dma((2,)),
             dma((2,)),
-            dma((8,)),
-            dma((8,)),
-            dma,
+            dma((2,)),
+            dma((2,)),
+            dma((2, 8)),
+            dma((2, 8)),
+            dma((2,)),
         ],
         compiler_params=pltpu.CompilerParams(
             collective_id=0, has_side_effects=True, vmem_limit_bytes=ROOT_MB * 1024 * 1024

time: 49.8 us -> 41.2 us (0.83)
  Pallas kernels: 49 us -> 40.2 us
    pallas_call x1, Pallas kernels: 42.1 us -> 33.3 us  [shards(): pl.pallas_call(functools.partial(root_kernel, rows), name='root', out_sha...]
where the time goes in v2:
time: 41.2 us; the launch traced here: 41 us
  Pallas kernels  40.2 us (98%)
  between operations  0.85 us (2%)
    pallas_call x1, Pallas kernels, shards(): pl.pallas_call(functools.partial(root_kernel, rows), name='root', out_sha...  33.3 us
    pallas_call x1, Pallas kernels, shards(): pl.pallas_call(fine_kernel, name='fine', grid=(SLOTS // TB,), out_shape=(...  6.92 us

profile of v2, /device:TPU:96, one launch (start us, length us, event | category | flops | bytes accessed | tf_op | source)
XLA Modules:
  0.0 41.0 jit_solution(2874687464364338848)
XLA Ops:
  0.6 0.0 copy-start.2
  0.6 0.0 copy-start.1
  0.7 0.0 copy-start
  0.7 33.3 %root.1 = (bf16[120,64,512]{2,1,0:T(8,128)(2,1)S(1)}, bf16[7680,128]{1,0:T(8,128)(2,1)S(1)}, bf16[2,8,128,128]{3,2,1,0:T(8,128)(2,1)S(1)}, bf16[32,4,32,32]{3,2,1,0:T(8,128)(2,1)S(1)}) custom-call(s32[1,120]{1,0:T(1,128)} %bitcast.8, s32[1,8]{1,0:T(1,128)} %bitcast.10, bf16[120,64,512]{2,1,0:T(8,128)(2,1)} %x_hbm.1, bf16[64,128]{1,0:T(8,128)(2,1)} %wp_hbm.1, ...), custom_call_target="tpu_custom_call" | custom-call | tf_op jit(solution)/shard_map/root/pallas_call | solution.py:527
  33.9 0.0 copy-done.2
  33.9 0.0 copy-done.1
  34.0 0.0 copy-done
  34.0 6.9 %fine.1 = (bf16[120,64,512]{2,1,0:T(8,128)(2,1)}, bf16[32,4,32,32]{3,2,1,0:T(8,128)(2,1)}) custom-call(s32[120]{0:T(128)S(1)} %copy-done.2, bf16[120,64,512]{2,1,0:T(8,128)(2,1)S(1)} %get-tuple-element.6.x_ref, bf16[7680,128]{1,0:T(8,128)(2,1)S(1)} %get-tuple-element.7.hid_ref, bf16[2,8,128,128]{3,2,1,0:T(8,128)(2,1)S(1)} %get-tuple-element.8.back_ref, ...), custom_call_target="tpu_custom_call" | custom-call | tf_op jit(solution)/shard_map/fine/pallas_call | solution.py:587
Async XLA Ops:
  0.6 33.3 %copy-start.2 = (s32[120]{0:T(128)S(1)}, s32[120]{0:T(128)}, u32[]{:S(2)}) copy-start(s32[120]{0:T(128)} %child_ref.1) | copy-start | bytes 1444
  0.6 33.3 %copy-start.1 = (bf16[128,64]{0,1:T(8,128)(2,1)S(1)}, bf16[128,64]{0,1:T(8,128)(2,1)}, u32[]{:S(2)}) copy-start(bf16[128,64]{0,1:T(8,128)(2,1)} %param.17) | copy-start | bytes 49156
  0.7 33.3 %copy-start = (bf16[256,128]{1,0:T(8,128)(2,1)S(1)}, bf16[256,128]{1,0:T(8,128)(2,1)}, u32[]{:S(2)}) copy-start(bf16[256,128]{1,0:T(8,128)(2,1)} %wd_ref.1) | copy-start | bytes 196612

commit v3 on v2

--- a/solution.py
+++ b/solution.py
@@ -67,12 +67,15 @@
     wc_ref,
     bias_ref,
     p8,
+    wp4,
     pp,
     ints,
     gathered,
     place,
     slab,
     halo,
+    halo_out,
+    own,
     weff,
     taps,
     rft,
@@ -90,8 +93,6 @@
     fw_recv,
     halo_send,
     halo_recv,
-    swap_send,
-    swap_recv,
     back_send,
     back_recv,
     own_sem,
@@ -144,16 +145,17 @@
     def _():
         pl.semaphore_signal(barrier, inc=1, device_id=(row + 1, me), device_id_type=MESH)
 
-    where = column_of(iota((512, 256), 0))
-    lane = iota((512, 256), 1)
-    for k in range(4):
-        p8[k * 512 : (k + 1) * 512] = jnp.where(lane == where + 64 * k, 0.125, 0.0).astype(BF)
+    hot = column_of(iota((1, 512), 1)) == iota((64, 512), 0)
+    p8[...] = jnp.where(hot, 0.125, 0.0).astype(BF)
+    wp4[...] = jnp.zeros((256, 512), BF)
     small[0].wait()
     small[1].wait()
     ints[me] = jnp.full((8, 128), -1, I32)
     ints[me, 0:1, 0:SLOTS] = child_ref[...]
     ints[me, 1:2, 0:8] = block_ref[...]
     small[2].wait()
+    for k in range(4):
+        wp4[k * 64 : (k + 1) * 64, k * 128 : (k + 1) * 128] = wp_ref[...]
 
     int_copies, ag_sent, fw_copies = [], [], []
 
@@ -176,7 +178,7 @@
         ag_sent.append(c)
 
     right, left, far = chip_peer(1), chip_peer(3), chip_peer(2)
-    relays = {1: (0, right), 2: (1, left)}
+    relays = {0: (0, right), 1: (1, left), 2: (0, right), 3: (1, left)}
     origin = (left, right, far)
 
     def arrived(blk, k):
@@ -190,20 +192,16 @@
 
     for blk, (first, n, sent) in enumerate(BLOCKS):
         x_copies[blk].wait()
-        x = jnp.concatenate(
-            [
-                jnp.concatenate([x_ref[first + 4 * g + k] for k in range(4)], axis=1)
-                for g in range(n // 4)
-            ],
-            axis=0,
+        x = x_ref[first : first + n].reshape(n * 64, 512)
+        pooled = nt(p8[...], x).astype(BF)
+        pooled = jnp.concatenate(
+            [pooled[:, g * 256 : (g + 1) * 256] for g in range(n // 4)], axis=0
         )
-        pooled = mm(x, p8[...]).astype(BF)
-        for g in range(n // 4):
-            h = tn(pooled[g * 64 : (g + 1) * 64], wp_ref[...])
-            h = jnp.maximum(h, 0.0).astype(BF)
-            hid_ref[pl.ds((first + 4 * g) * 64, 256), :] = h
-            mean = jnp.sum(h.astype(F32).reshape(4, 8, 8, 128), axis=1) * 0.125
-            pp[pl.ds(g * 32, 32), :] = mean.reshape(32, 128)
+        h4 = jnp.maximum(mm(pooled, wp4[...]), 0.0).astype(BF)
+        for t in range(n):
+            h = h4[t // 4 * 64 : t // 4 * 64 + 64, t % 4 * 128 : t % 4 * 128 + 128]
+            hid_ref[pl.ds((first + t) * 64, 64), :] = h
+            pp[pl.ds(t * 8, 8), :] = jnp.sum(h.astype(F32).reshape(8, 8, 128), axis=0) * 0.125
         if n < sent:
             pp[pl.ds(n * 8, (sent - n) * 8), :] = jnp.zeros(((sent - n) * 8, 128), F32)
         start = pl.multiple_of(me * 128 + first, 16)
@@ -224,8 +222,8 @@
                 c = remote(ints.at[me], ints.at[me], int_send.at[k], int_recv.at[k], row, peer(k))
                 c.start()
                 int_copies.append(c)
-        if blk >= 3:
-            arrived(blk - 2, relays[blk - 2][0])
+        if blk == 4:
+            arrived(0, relays[0][0])
 
     for c in small[3:]:
         c.wait()
@@ -252,64 +250,35 @@
     for m in range(8):
         hot = iota((512, 128), 0) == pos[m : m + 1, :]
         place[:, m * 128 : (m + 1) * 128] = jnp.where(hot, 1.0, 0.0).astype(BF)
-    for blk in range(NB):
-        for k in (0, 1, 2):
-            if blk not in relays or relays[blk][0] != k:
-                arrived(blk, k)
+    order = [(b, k) for b in range(NB) for k in (0, 1)]
+    order += [(b, 2) for b in (0, 1, 4, 2, 3)]
+    for blk, k in order:
+        if (blk, k) != (0, relays[0][0]):
+            arrived(blk, k)
     for c in fw_copies:
         c.wait_recv()
 
     def put(half, i):
         r = pl.ds(half * 256, 256)
-        c = slice(i * 256, (i + 1) * 256)
+        c = slice(i * 512, (i + 1) * 512)
         slab[r, c] = mm(place[r, :], gathered[:, c]).astype(BF)
 
-    near = pl.ds(pl.multiple_of(core * 256, 256), 256)
     low = remote(
-        slab.at[pl.ds(0, 256), near],
-        halo.at[1, core],
+        halo_out.at[0],
+        halo.at[1],
         halo_send.at[0],
         halo_recv.at[1],
         jnp.maximum(row - 1, 0),
         me,
     )
     high = remote(
-        slab.at[pl.ds(256, 256), pl.ds(pl.multiple_of(512 + core * 256, 256), 256)],
-        halo.at[0, core],
+        halo_out.at[1],
+        halo.at[0],
         halo_send.at[1],
         halo_recv.at[0],
         jnp.minimum(row + 1, last),
         me,
     )
-    swaps = [
-        remote(
-            halo.at[side, core],
-            halo.at[side, core],
-            swap_send.at[side],
-            swap_recv.at[side],
-            row,
-            partner,
-        )
-        for side in range(2)
-    ]
-    put(0, 0)
-    put(0, 1)
-
-    @pl.when(row > 0)
-    def _():
-        low.start()
-
-    put(1, 2)
-    put(1, 3)
-
-    @pl.when(row < last)
-    def _():
-        high.start()
-
-    put(0, 2)
-    put(0, 3)
-    put(1, 0)
-    put(1, 1)
 
     spot = iota((32, 256), 1)
     oy, ox = spot >> 4, spot & 15
@@ -327,16 +296,20 @@
         return jnp.concatenate([weff[d * 288 : (d + 1) * 288] for d in range(lo, hi)], axis=1)
 
     def matmuls(z):
-        lo, hi = max(0, 1 - z), min(3, 5 - z)
-        for ab in range(4):
-            x = jnp.concatenate([plane(z - 1 + d, ab) for d in range(lo, hi)], axis=1)
-            taps[z, ab] = nt(weights(lo, hi), x)
-
-    def outer(z, side, half):
-        d = 0 if side == 0 else 2
-        for i in range(2):
-            x = halo[side, half, :, i * 128 : (i + 1) * 128]
-            taps[z, 2 * half + i] += nt(weights(d, d + 1), x)
+        if z == 4:
+            ds, zs = (2, 3), [0]
+        elif z == 5:
+            ds, zs = (0, 1), [3]
+        else:
+            ds = (max(0, 1 - z), min(3, 5 - z))
+            zs = [z - 1 + d for d in range(*ds)]
+        for a in range(2):
+            x = [
+                jnp.concatenate([plane(zz, 2 * a + b) for zz in zs], axis=1) for b in range(2)
+            ]
+            r = nt(weights(*ds), jnp.concatenate(x, axis=0))
+            taps[z, 2 * a] = r[:, :256]
+            taps[z, 2 * a + 1] = r[:, 256:]
 
     def combine(z):
         def tap(a, b, dy, dx):
@@ -363,20 +336,28 @@
                     return jnp.where(oy == (15 if iy else 0), 0.0, v)
 
                 total = plain + shift_x(only_x) + shift_y(only_y + shift_x(both))
-                out = jnp.maximum(total + bias, 0.0).astype(BF)
-                r = (iy * 2 + ix) * 32
-                part = 0 if z in (1, 2) else 1
-                rft[part, r : r + 32, (z >> 1) * 256 : ((z >> 1) + 1) * 256] = out
-                r = iy * 128 + z * 32
-                quad[r : r + 32, ix * 256 : (ix + 1) * 256] = out
+                if z >= 4:
+                    halo_out[z - 4, iy * 2 + ix] = total.astype(BF)
+                elif z in (0, 3):
+                    own[z // 3, iy * 2 + ix] = total + bias
+                else:
+                    finish(z, iy, ix, total + bias)
+
+    def finish(z, iy, ix, total):
+        out = jnp.maximum(total, 0.0).astype(BF)
+        r = (iy * 2 + ix) * 32
+        part = 0 if z in (1, 2) else 1
+        rft[part, r : r + 32, (z >> 1) * 256 : ((z >> 1) + 1) * 256] = out
+        r = iy * 128 + z * 32
+        quad[r : r + 32, ix * 256 : (ix + 1) * 256] = out
 
     back_copies, own_copies = [], []
 
     def give_back(part):
-        for i in range(4):
-            m2 = mm(rft[part], place[:, i * 256 : (i + 1) * 256]).astype(BF)
-            msgs[part, 2 * i] = m2[:, :128]
-            msgs[part, 2 * i + 1] = m2[:, 128:]
+        for i in range(2):
+            m4 = mm(rft[part], place[:, i * 512 : (i + 1) * 512]).astype(BF)
+            for t in range(4):
+                msgs[part, 4 * i + t] = m4[:, t * 128 : (t + 1) * 128]
         for k in (4, 3, 5, 2, 6, 1, 7):
             c = remote(
                 msgs.at[part, peer(k)],
@@ -394,12 +375,30 @@
 
     @pl.when(row == 0)
     def _():
-        halo[0] = jnp.zeros((2, 256, 256), BF)
+        halo[0] = jnp.zeros((4, 32, 256), BF)
 
     @pl.when(row == last)
     def _():
-        halo[1] = jnp.zeros((2, 256, 256), BF)
-
+        halo[1] = jnp.zeros((4, 32, 256), BF)
+
+    put(0, 0)
+    matmuls(4)
+    combine(4)
+
+    @pl.when(row > 0)
+    def _():
+        low.start()
+
+    put(1, 1)
+    matmuls(5)
+    combine(5)
+
+    @pl.when(row < last)
+    def _():
+        high.start()
+
+    put(0, 1)
+    put(1, 0)
     matmuls(1)
     matmuls(2)
     combine(1)
@@ -407,35 +406,25 @@
     give_back(0)
     matmuls(0)
     matmuls(3)
-    p, q = iota((512, 512), 0), iota((512, 512), 1)
-    hot = q == ((p >> 4) & 15) * 32 + 2 * (p & 15) + (p >> 8)
-    perm[...] = jnp.where(hot, 1.0, 0.0).astype(BF)
-
-    @pl.when(row > 0)
-    def _():
-        high.wait_recv()
-        swaps[0].start()
-
-    @pl.when(row < last)
-    def _():
-        low.wait_recv()
-        swaps[1].start()
-
-    outer(0, 0, core)
-    outer(3, 1, core)
-
-    @pl.when(row > 0)
-    def _():
-        swaps[0].wait_recv()
-
-    @pl.when(row < last)
-    def _():
-        swaps[1].wait_recv()
-
-    outer(0, 0, 1 - core)
-    outer(3, 1, 1 - core)
     combine(0)
     combine(3)
+    p, q = iota((512, 1), 0), iota((512, 512), 1)
+    spread = ((p >> 4) & 15) * 32 + 2 * (p & 15) + (p >> 8)
+    perm[...] = jnp.where(q == spread, 1.0, 0.0).astype(BF)
+
+    @pl.when(row > 0)
+    def _():
+        high.wait_recv()
+
+    @pl.when(row < last)
+    def _():
+        low.wait_recv()
+
+    for z in (0, 3):
+        for iy in range(2):
+            for ix in range(2):
+                c = iy * 2 + ix
+                finish(z, iy, ix, own[z // 3, c] + halo[z // 3, c].astype(F32))
     give_back(1)
 
     nat = mm(quad[...], perm[...])
@@ -459,12 +448,10 @@
     @pl.when(row > 0)
     def _():
         low.wait_send()
-        swaps[0].wait_send()
 
     @pl.when(row < last)
     def _():
         high.wait_send()
-        swaps[1].wait_send()
 
     for c in own_copies:
         c.wait()
@@ -481,7 +468,7 @@
     @pl.when(step == 0)
     def _():
         copy.start()
-        where = column_of(iota((256, 512), 1))
+        where = column_of(iota((1, 512), 1))
         line = iota((256, 512), 0)
         for k in range(4):
             up[k] = jnp.where(line == where + 64 * k, 1.0, 0.0).astype(BF)
@@ -542,15 +529,18 @@
             pltpu.VMEM((128, 256), BF),
             pltpu.VMEM((864, 256), BF),
             pltpu.VMEM((1, 32), F32),
-            pltpu.VMEM((2048, 256), BF),
+            pltpu.VMEM((64, 512), BF),
+            pltpu.VMEM((256, 512), BF),
             pltpu.VMEM((256, 128), F32),
             pltpu.VMEM((8, 8, 128), I32),
             pltpu.VMEM((1024, 1024), BF),
             pltpu.VMEM((512, 1024), BF),
             pltpu.VMEM((512, 1024), BF),
-            pltpu.VMEM((2, 2, 256, 256), BF),
+            pltpu.VMEM((2, 4, 32, 256), BF),
+            pltpu.VMEM((2, 4, 32, 256), BF),
+            pltpu.VMEM((2, 4, 32, 256), F32),
             pltpu.VMEM((864, 128), BF),
-            pltpu.VMEM((4, 4, 288, 256), F32),
+            pltpu.VMEM((6, 4, 288, 256), F32),
             pltpu.VMEM((2, 128, 512), BF),
             pltpu.VMEM((256, 512), BF),
             pltpu.VMEM((512, 512), BF),
@@ -564,8 +554,6 @@
             dma((NB, 3)),
             dma((NB, 4)),
             dma((NB, 4)),
-            dma((2,)),
-            dma((2,)),
             dma((2,)),
             dma((2,)),
             dma((2, 8)),

time: 41.2 us -> 38.1 us (0.925)
  Pallas kernels: 40.2 us -> 37.1 us
    pallas_call x1, Pallas kernels: 33.3 us -> 30.1 us  [shards(): pl.pallas_call(functools.partial(root_kernel, rows), name='root', out_sha...]
where the time goes in v3:
time: 38.1 us; the launch traced here: 37.8 us
  Pallas kernels  37.1 us (97%)
  between operations  0.69 us (2%)
    pallas_call x1, Pallas kernels, shards(): pl.pallas_call(functools.partial(root_kernel, rows), name='root', out_sha...  30.1 us
    pallas_call x1, Pallas kernels, shards(): pl.pallas_call(fine_kernel, name='fine', grid=(SLOTS // TB,), out_shape=(...  6.91 us

profile of v3, /device:TPU:96, one launch (start us, length us, event | category | flops | bytes accessed | tf_op | source)
XLA Modules:
  0.0 37.8 jit_solution(1109691696543316897)
XLA Ops:
  0.6 0.0 copy-start.2
  0.6 0.0 copy-start.1
  0.7 0.0 copy-start
  0.7 30.1 %root.1 = (bf16[120,64,512]{2,1,0:T(8,128)(2,1)S(1)}, bf16[7680,128]{1,0:T(8,128)(2,1)S(1)}, bf16[2,8,128,128]{3,2,1,0:T(8,128)(2,1)S(1)}, bf16[32,4,32,32]{3,2,1,0:T(8,128)(2,1)S(1)}) custom-call(s32[1,120]{1,0:T(1,128)} %bitcast.8, s32[1,8]{1,0:T(1,128)} %bitcast.10, bf16[120,64,512]{2,1,0:T(8,128)(2,1)} %x_hbm.1, bf16[64,128]{1,0:T(8,128)(2,1)} %wp_hbm.1, ...), custom_call_target="tpu_custom_call" | custom-call | tf_op jit(solution)/shard_map/root/pallas_call | solution.py:514
  30.8 0.0 copy-done.2
  30.8 0.0 copy-done.1
  30.8 0.0 copy-done
  30.8 6.9 %fine.1 = (bf16[120,64,512]{2,1,0:T(8,128)(2,1)}, bf16[32,4,32,32]{3,2,1,0:T(8,128)(2,1)}) custom-call(s32[120]{0:T(128)S(1)} %copy-done.2, bf16[120,64,512]{2,1,0:T(8,128)(2,1)S(1)} %get-tuple-element.6.x_ref, bf16[7680,128]{1,0:T(8,128)(2,1)S(1)} %get-tuple-element.7.hid_ref, bf16[2,8,128,128]{3,2,1,0:T(8,128)(2,1)S(1)} %get-tuple-element.8.back_ref, ...), custom_call_target="tpu_custom_call" | custom-call | tf_op jit(solution)/shard_map/fine/pallas_call | solution.py:575
Async XLA Ops:
  0.6 30.2 %copy-start.2 = (s32[120]{0:T(128)S(1)}, s32[120]{0:T(128)}, u32[]{:S(2)}) copy-start(s32[120]{0:T(128)} %child_ref.1) | copy-start | bytes 1444
  0.6 30.2 %copy-start.1 = (bf16[128,64]{0,1:T(8,128)(2,1)S(1)}, bf16[128,64]{0,1:T(8,128)(2,1)}, u32[]{:S(2)}) copy-start(bf16[128,64]{0,1:T(8,128)(2,1)} %param.17) | copy-start | bytes 49156
  0.7 30.2 %copy-start = (bf16[256,128]{1,0:T(8,128)(2,1)S(1)}, bf16[256,128]{1,0:T(8,128)(2,1)}, u32[]{:S(2)}) copy-start(bf16[256,128]{1,0:T(8,128)(2,1)} %wd_ref.1) | copy-start | bytes 196612

commit v4 on v3

--- a/solution.py
+++ b/solution.py
@@ -14,7 +14,7 @@
 SLOTS = 120
 BLOCKS = ((0, 16, 16), (16, 32, 32), (48, 32, 32), (80, 32, 32), (112, 8, 16))
 NB = len(BLOCKS)
-TB = 24
+PARTS = ((0, 32), (32, 32), (64, 24), (88, 16), (104, 16))
 OUT = jax.ShapeDtypeStruct
 ROOT_MB = 40
 FINE_MB = 24
@@ -178,7 +178,7 @@
         ag_sent.append(c)
 
     right, left, far = chip_peer(1), chip_peer(3), chip_peer(2)
-    relays = {0: (0, right), 1: (1, left), 2: (0, right), 3: (1, left)}
+    relays = {0: (0, right), 1: (1, left), 2: (0, right), 3: (1, left), 4: (0, right)}
     origin = (left, right, far)
 
     def arrived(blk, k):
@@ -251,7 +251,7 @@
         hot = iota((512, 128), 0) == pos[m : m + 1, :]
         place[:, m * 128 : (m + 1) * 128] = jnp.where(hot, 1.0, 0.0).astype(BF)
     order = [(b, k) for b in range(NB) for k in (0, 1)]
-    order += [(b, 2) for b in (0, 1, 4, 2, 3)]
+    order += [(b, 2) for b in range(NB)]
     for blk, k in order:
         if (blk, k) != (0, relays[0][0]):
             arrived(blk, k)
@@ -460,46 +460,58 @@
 
 
 def fine_kernel(
-    child_ref, x_ref, hid_ref, back_ref, wd_ref, ws_ref, feat_ref, out_ref, root_ref, up, lifted, sem
+    child_ref,
+    x_ref,
+    hid_ref,
+    back_ref,
+    wd_ref,
+    ws_ref,
+    feat_ref,
+    out_hbm,
+    root_hbm,
+    up,
+    lifted,
+    out_ref,
+    out_sem,
+    root_sem,
 ):
-    step = pl.program_id(0)
-    copy = pltpu.make_async_copy(feat_ref, root_ref, sem)
-
-    @pl.when(step == 0)
-    def _():
-        copy.start()
-        where = column_of(iota((1, 512), 1))
-        line = iota((256, 512), 0)
+    root_copy = pltpu.make_async_copy(feat_ref, root_hbm, root_sem)
+    root_copy.start()
+    where = column_of(iota((1, 512), 1))
+    line = iota((128, 512), 0)
+    for k in range(2):
+        up[k] = jnp.where(line == where + 64 * k, 1.0, 0.0).astype(BF)
+    for i in range(8):
+        rows = slice(i % 4 * 32, i % 4 * 32 + 32)
+        r = jnp.concatenate([back_ref[i // 4, j, rows, :] for j in range(8)], axis=0)
+        lifted[i * 128 : (i + 1) * 128, :] = tn(r, wd_ref[...])
+
+    copies = []
+    for part, (first, count) in enumerate(PARTS):
+        skips = []
+        for g in range(count // 4):
+            dec = []
+            for k in range(4):
+                s = first + 4 * g + k
+                child = child_ref[s]
+                lift = lifted[pl.ds(s, 8, stride=128), :]
+                lift = jnp.where((child >> 2) & 1 == 0, pltpu.roll(lift, 4, 0), lift)
+                lift = jnp.where(child >= 0, lift, -3e38)
+                h = hid_ref[pl.ds(s * 64, 64), :].astype(F32).reshape(8, 8, 128)
+                dec.append(jnp.maximum(h + lift[None], 0.0).reshape(64, 128).astype(BF))
+            skips.append(nt(ws_ref[...], jnp.concatenate(dec, axis=0)).astype(BF))
+        skip = jnp.concatenate(skips, axis=0)
         for k in range(4):
-            up[k] = jnp.where(line == where + 64 * k, 1.0, 0.0).astype(BF)
-        for i in range(8):
-            rows = slice(i % 4 * 32, i % 4 * 32 + 32)
-            r = jnp.concatenate([back_ref[i // 4, j, rows, :] for j in range(8)], axis=0)
-            lifted[i * 128 : (i + 1) * 128, :] = tn(r, wd_ref[...])
-
-    skips = []
-    for g in range(TB // 4):
-        dec = []
-        for k in range(4):
-            s = step * TB + 4 * g + k
-            child = child_ref[s]
-            lift = lifted[pl.ds(s, 8, stride=128), :]
-            lift = jnp.where((child >> 2) & 1 == 0, pltpu.roll(lift, 4, 0), lift)
-            lift = jnp.where(child >= 0, lift, -3e38)
-            h = hid_ref[pl.ds(pl.multiple_of(s * 64, 64), 64), :].astype(F32).reshape(8, 8, 128)
-            dec.append(jnp.maximum(h + lift[None], 0.0).reshape(64, 128).astype(BF))
-        skips.append(nt(ws_ref[...], jnp.concatenate(dec, axis=0)).astype(BF))
-    skip = jnp.concatenate(skips, axis=0)
-    for k in range(4):
-        r = mm(skip, up[k])
-        for g in range(TB // 4):
-            s = 4 * g + k
-            x = x_ref[step * TB + s].astype(F32)
-            out_ref[s] = (x + r[g * 64 : (g + 1) * 64]).astype(BF)
-
-    @pl.when(step == SLOTS // TB - 1)
-    def _():
-        copy.wait()
+            r = mm(skip[:, k // 2 * 128 : k // 2 * 128 + 128], up[k % 2])
+            for g in range(count // 4):
+                s = first + 4 * g + k
+                out_ref[s] = (x_ref[s].astype(F32) + r[g * 64 : (g + 1) * 64]).astype(BF)
+        span = pl.ds(first, count)
+        copies.append(pltpu.make_async_copy(out_ref.at[span], out_hbm.at[span], out_sem.at[part]))
+        copies[-1].start()
+    for c in copies:
+        c.wait()
+    root_copy.wait()
 
 
 def shards(
@@ -575,17 +587,18 @@
     return pl.pallas_call(
         fine_kernel,
         name="fine",
-        grid=(SLOTS // TB,),
         out_shape=(
             jax.ShapeDtypeStruct((SLOTS, 64, 512), BF),
             jax.ShapeDtypeStruct((32, 4, 32, 32), BF),
         ),
         in_specs=[pl.BlockSpec(memory_space=pltpu.SMEM), vm, vm, vm, vm, vm, anym],
-        out_specs=(pl.BlockSpec((TB, 64, 512), lambda i: (i, 0, 0)), anym),
+        out_specs=(hbm, hbm),
         scratch_shapes=[
-            pltpu.VMEM((4, 256, 512), BF),
+            pltpu.VMEM((2, 128, 512), BF),
             pltpu.VMEM((1024, 128), F32),
-            pltpu.SemaphoreType.DMA,
+            pltpu.VMEM((SLOTS, 64, 512), BF),
+            dma((len(PARTS),)),
+            dma,
         ],
         compiler_params=pltpu.CompilerParams(vmem_limit_bytes=FINE_MB * 1024 * 1024),
     )(fine_child, x, hidden, back, w_down, w_skip.T, feat)

time: 38.1 us -> 36.1 us (0.948)
  Pallas kernels: 37.1 us -> 35 us
    pallas_call x1, Pallas kernels: 6.91 us -> 5.35 us  [shards(): pl.pallas_call(fine_kernel, name='fine', out_shape=(jax.ShapeDtypeStruct(...]
    pallas_call x1, Pallas kernels: 30.1 us -> 29.7 us  [shards(): pl.pallas_call(functools.partial(root_kernel, rows), name='root', out_sha...]
where the time goes in v4:
time: 36.1 us; the launch traced here: 35.7 us
  Pallas kernels  35 us (97%)
  between operations  0.69 us (2%)
    pallas_call x1, Pallas kernels, shards(): pl.pallas_call(functools.partial(root_kernel, rows), name='root', out_sha...  29.7 us
    pallas_call x1, Pallas kernels, shards(): pl.pallas_call(fine_kernel, name='fine', out_shape=(jax.ShapeDtypeStruct(...  5.35 us

profile of v4, /device:TPU:96, one launch (start us, length us, event | category | flops | bytes accessed | tf_op | source)
XLA Modules:
  0.0 35.7 jit_solution(6181923604483679962)
XLA Ops:
  0.6 0.0 copy-start.2
  0.6 0.0 copy-start.1
  0.7 0.0 copy-start
  0.7 29.7 %root.1 = (bf16[120,64,512]{2,1,0:T(8,128)(2,1)S(1)}, bf16[7680,128]{1,0:T(8,128)(2,1)S(1)}, bf16[2,8,128,128]{3,2,1,0:T(8,128)(2,1)S(1)}, bf16[32,4,32,32]{3,2,1,0:T(8,128)(2,1)S(1)}) custom-call(s32[1,120]{1,0:T(1,128)} %bitcast.8, s32[1,8]{1,0:T(1,128)} %bitcast.10, bf16[120,64,512]{2,1,0:T(8,128)(2,1)} %x_hbm.1, bf16[64,128]{1,0:T(8,128)(2,1)} %wp_hbm.1, ...), custom_call_target="tpu_custom_call" | custom-call | tf_op jit(solution)/shard_map/root/pallas_call | solution.py:526
  30.4 0.0 copy-done.2
  30.4 0.0 copy-done.1
  30.4 0.0 copy-done
  30.4 5.4 %fine.1 = (bf16[120,64,512]{2,1,0:T(8,128)(2,1)}, bf16[32,4,32,32]{3,2,1,0:T(8,128)(2,1)}) custom-call(s32[120]{0:T(128)S(1)} %copy-done.2, bf16[120,64,512]{2,1,0:T(8,128)(2,1)S(1)} %get-tuple-element.6.x_ref, bf16[7680,128]{1,0:T(8,128)(2,1)S(1)} %get-tuple-element.7.hid_ref, bf16[2,8,128,128]{3,2,1,0:T(8,128)(2,1)S(1)} %get-tuple-element.8.back_ref, ...), custom_call_target="tpu_custom_call" | custom-call | tf_op jit(solution)/shard_map/fine/pallas_call | solution.py:587
Async XLA Ops:
  0.6 29.7 %copy-start.2 = (s32[120]{0:T(128)S(1)}, s32[120]{0:T(128)}, u32[]{:S(2)}) copy-start(s32[120]{0:T(128)} %child_ref.1) | copy-start | bytes 1444
  0.6 29.7 %copy-start.1 = (bf16[128,64]{0,1:T(8,128)(2,1)S(1)}, bf16[128,64]{0,1:T(8,128)(2,1)}, u32[]{:S(2)}) copy-start(bf16[128,64]{0,1:T(8,128)(2,1)} %param.17) | copy-start | bytes 49156
  0.7 29.7 %copy-start = (bf16[256,128]{1,0:T(8,128)(2,1)S(1)}, bf16[256,128]{1,0:T(8,128)(2,1)}, u32[]{:S(2)}) copy-start(bf16[256,128]{1,0:T(8,128)(2,1)} %wd_ref.1) | copy-start | bytes 196612

commit v5 on v4

--- a/solution.py
+++ b/solution.py
@@ -14,7 +14,7 @@
 SLOTS = 120
 BLOCKS = ((0, 16, 16), (16, 32, 32), (48, 32, 32), (80, 32, 32), (112, 8, 16))
 NB = len(BLOCKS)
-PARTS = ((0, 32), (32, 32), (64, 24), (88, 16), (104, 16))
+PARTS = ((0, 8),) + tuple((8 + 16 * i, 16) for i in range(7))
 OUT = jax.ShapeDtypeStruct
 ROOT_MB = 40
 FINE_MB = 24
@@ -382,16 +382,15 @@
         halo[1] = jnp.zeros((4, 32, 256), BF)
 
     put(0, 0)
+    put(1, 1)
     matmuls(4)
+    matmuls(5)
     combine(4)
+    combine(5)
 
     @pl.when(row > 0)
     def _():
         low.start()
-
-    put(1, 1)
-    matmuls(5)
-    combine(5)
 
     @pl.when(row < last)
     def _():

time: 36.1 us -> 35.5 us (0.983)
  Pallas kernels: 35 us -> 34.4 us
    pallas_call x1, Pallas kernels: 29.7 us -> 29 us  [shards(): pl.pallas_call(functools.partial(root_kernel, rows), name='root', out_sha...]
where the time goes in v5:
time: 35.5 us; the launch traced here: 35.1 us
  Pallas kernels  34.4 us (97%)
  between operations  0.69 us (2%)
    pallas_call x1, Pallas kernels, shards(): pl.pallas_call(functools.partial(root_kernel, rows), name='root', out_sha...  29 us
    pallas_call x1, Pallas kernels, shards(): pl.pallas_call(fine_kernel, name='fine', out_shape=(jax.ShapeDtypeStruct(...  5.42 us

profile of v5, /device:TPU:96, one launch (start us, length us, event | category | flops | bytes accessed | tf_op | source)
XLA Modules:
  0.0 35.1 jit_solution(15014230868630968074)
XLA Ops:
  0.6 0.0 copy-start.2
  0.6 0.0 copy-start.1
  0.7 0.0 copy-start
  0.7 29.0 %root.1 = (bf16[120,64,512]{2,1,0:T(8,128)(2,1)S(1)}, bf16[7680,128]{1,0:T(8,128)(2,1)S(1)}, bf16[2,8,128,128]{3,2,1,0:T(8,128)(2,1)S(1)}, bf16[32,4,32,32]{3,2,1,0:T(8,128)(2,1)S(1)}) custom-call(s32[1,120]{1,0:T(1,128)} %bitcast.8, s32[1,8]{1,0:T(1,128)} %bitcast.10, bf16[120,64,512]{2,1,0:T(8,128)(2,1)} %x_hbm.1, bf16[64,128]{1,0:T(8,128)(2,1)} %wp_hbm.1, ...), custom_call_target="tpu_custom_call" | custom-call | tf_op jit(solution)/shard_map/root/pallas_call | solution.py:525
  29.7 0.0 copy-done.2
  29.7 0.0 copy-done.1
  29.7 0.0 copy-done
  29.7 5.4 %fine.1 = (bf16[120,64,512]{2,1,0:T(8,128)(2,1)}, bf16[32,4,32,32]{3,2,1,0:T(8,128)(2,1)}) custom-call(s32[120]{0:T(128)S(1)} %copy-done.2, bf16[120,64,512]{2,1,0:T(8,128)(2,1)S(1)} %get-tuple-element.6.x_ref, bf16[7680,128]{1,0:T(8,128)(2,1)S(1)} %get-tuple-element.7.hid_ref, bf16[2,8,128,128]{3,2,1,0:T(8,128)(2,1)S(1)} %get-tuple-element.8.back_ref, ...), custom_call_target="tpu_custom_call" | custom-call | tf_op jit(solution)/shard_map/fine/pallas_call | solution.py:586
Async XLA Ops:
  0.6 29.1 %copy-start.2 = (s32[120]{0:T(128)S(1)}, s32[120]{0:T(128)}, u32[]{:S(2)}) copy-start(s32[120]{0:T(128)} %child_ref.1) | copy-start | bytes 1444
  0.6 29.1 %copy-start.1 = (bf16[128,64]{0,1:T(8,128)(2,1)S(1)}, bf16[128,64]{0,1:T(8,128)(2,1)}, u32[]{:S(2)}) copy-start(bf16[128,64]{0,1:T(8,128)(2,1)} %param.17) | copy-start | bytes 49156
  0.7 29.1 %copy-start = (bf16[256,128]{1,0:T(8,128)(2,1)S(1)}, bf16[256,128]{1,0:T(8,128)(2,1)}, u32[]{:S(2)}) copy-start(bf16[256,128]{1,0:T(8,128)(2,1)} %wd_ref.1) | copy-start | bytes 196612

commit v6 on v5

--- a/solution.py
+++ b/solution.py
@@ -12,7 +12,7 @@
 I32 = jnp.int32
 MESH = pl.DeviceIdType.MESH
 SLOTS = 120
-BLOCKS = ((0, 16, 16), (16, 32, 32), (48, 32, 32), (80, 32, 32), (112, 8, 16))
+BLOCKS = ((0, 16, 16), (16, 32, 32), (48, 32, 32), (80, 16, 16), (96, 16, 16), (112, 8, 16))
 NB = len(BLOCKS)
 PARTS = ((0, 8),) + tuple((8 + 16 * i, 16) for i in range(7))
 OUT = jax.ShapeDtypeStruct
@@ -178,7 +178,7 @@
         ag_sent.append(c)
 
     right, left, far = chip_peer(1), chip_peer(3), chip_peer(2)
-    relays = {0: (0, right), 1: (1, left), 2: (0, right), 3: (1, left), 4: (0, right)}
+    relays = {b: (b % 2, left if b % 2 else right) for b in range(NB)}
     origin = (left, right, far)
 
     def arrived(blk, k):

time: 35.5 us -> 36.8 us (1.037)
  Pallas kernels: 34.4 us -> 35.8 us
    pallas_call x1, Pallas kernels: 29 us -> 30.4 us  [shards(): pl.pallas_call(functools.partial(root_kernel, rows), name='root', out_sha...]
where the time goes in v6:
time: 36.8 us; the launch traced here: 36.5 us
  Pallas kernels  35.8 us (97%)
  between operations  0.69 us (2%)
    pallas_call x1, Pallas kernels, shards(): pl.pallas_call(functools.partial(root_kernel, rows), name='root', out_sha...  30.4 us
    pallas_call x1, Pallas kernels, shards(): pl.pallas_call(fine_kernel, name='fine', out_shape=(jax.ShapeDtypeStruct(...  5.41 us

profile of v6, /device:TPU:96, one launch (start us, length us, event | category | flops | bytes accessed | tf_op | source)
XLA Modules:
  0.0 36.5 jit_solution(15494587728777071262)
XLA Ops:
  0.6 0.0 copy-start.2
  0.6 0.0 copy-start.1
  0.7 0.0 copy-start
  0.7 30.4 %root.1 = (bf16[120,64,512]{2,1,0:T(8,128)(2,1)S(1)}, bf16[7680,128]{1,0:T(8,128)(2,1)S(1)}, bf16[2,8,128,128]{3,2,1,0:T(8,128)(2,1)S(1)}, bf16[32,4,32,32]{3,2,1,0:T(8,128)(2,1)S(1)}) custom-call(s32[1,120]{1,0:T(1,128)} %bitcast.8, s32[1,8]{1,0:T(1,128)} %bitcast.10, bf16[120,64,512]{2,1,0:T(8,128)(2,1)} %x_hbm.1, bf16[64,128]{1,0:T(8,128)(2,1)} %wp_hbm.1, ...), custom_call_target="tpu_custom_call" | custom-call | tf_op jit(solution)/shard_map/root/pallas_call | solution.py:525
  31.0 0.0 copy-done.2
  31.0 0.0 copy-done.1
  31.1 0.0 copy-done
  31.1 5.4 %fine.1 = (bf16[120,64,512]{2,1,0:T(8,128)(2,1)}, bf16[32,4,32,32]{3,2,1,0:T(8,128)(2,1)}) custom-call(s32[120]{0:T(128)S(1)} %copy-done.2, bf16[120,64,512]{2,1,0:T(8,128)(2,1)S(1)} %get-tuple-element.6.x_ref, bf16[7680,128]{1,0:T(8,128)(2,1)S(1)} %get-tuple-element.7.hid_ref, bf16[2,8,128,128]{3,2,1,0:T(8,128)(2,1)S(1)} %get-tuple-element.8.back_ref, ...), custom_call_target="tpu_custom_call" | custom-call | tf_op jit(solution)/shard_map/fine/pallas_call | solution.py:586
Async XLA Ops:
  0.6 30.4 %copy-start.2 = (s32[120]{0:T(128)S(1)}, s32[120]{0:T(128)}, u32[]{:S(2)}) copy-start(s32[120]{0:T(128)} %child_ref.1) | copy-start | bytes 1444
  0.6 30.4 %copy-start.1 = (bf16[128,64]{0,1:T(8,128)(2,1)S(1)}, bf16[128,64]{0,1:T(8,128)(2,1)}, u32[]{:S(2)}) copy-start(bf16[128,64]{0,1:T(8,128)(2,1)} %param.17) | copy-start | bytes 49156
  0.7 30.4 %copy-start = (bf16[256,128]{1,0:T(8,128)(2,1)S(1)}, bf16[256,128]{1,0:T(8,128)(2,1)}, u32[]{:S(2)}) copy-start(bf16[256,128]{1,0:T(8,128)(2,1)} %wd_ref.1) | copy-start | bytes 196612
